TPU v7x, 32 devices: a whole 2x2x4 slice. The times are simulated.
32 devices in a mesh: tm: 4 (over z), sub: 8 (over y, x, core).
Axes of the slice: x: 2, y: 2, z: 4, core: 2. Of those that a mesh axis runs over, the one named last changes fastest.
Arguments:
- starts: float32 [4, 8, 16, 1024], P('tm', 'sub'), may hold values from -6 to 6
- inverses: float32 [8, 1024, 1024], P('sub')
- retain: float32 [8, 1024], P('sub'), may hold values from 0.4 to 1.1
- sources: float32 [8, 16, 1024], P('sub'), may hold values from -4 to 4
- coarse_decay: float32 [8, 1024], P('sub'), may hold values from 0.88 to 0.995
- admittance: float32 [8, 8], P('sub'), may hold values from 0.2 to 0.6
- partner: int32 [8, 8], P('sub'), may hold values from 0 to 63, as said below
- line_delay: int32 [8, 8], P('sub'), may hold values from 2 to 5, as said below
- line_live: int32 [8, 8], P('sub'), may hold values from 0 to 1, as said below
- term_block: int32 [8, 8], P('sub'), may hold values from 0 to 127, as said below
Outputs:
- ends: float32 [4, 8, 16, 1024], P('tm', 'sub')
Inputs may be any that keep to these rules, and one draw needn't show every extreme that they name: Slots are paired: partner[i] = k exactly when partner[k] = i. A slot may be its own partner; such a slot is out of service. Of the slots of one index d of sub (its 1 subnetworks), exactly 2 are their own partners, and the others have partners on exactly 3 other indices, 2 slots on each and none elsewhere; these indices are d + 4 and pairs d + s and d - s modulo the number of indices. `line_delay`: paired slots have equal delays. `line_live`: paired slots are both in service or both not. `term_block`: the slots of one subnetwork have distinct blocks.
All inputs are finite; a program needn't handle non-finite values.
Results may differ from a plain program's by a relative error of at most 0.0001.
Values sent between devices are 32-bit elements; how exact they have to be, the bound alone decides.
No kernel may reach another device: no remote copies, remote signals or barrier semaphores. Data moves between devices by JAX's collectives and lax.ppermute only.
A program may use at most 64 MiB of HBM per device.

v0:
```python
import jax
import jax.numpy as jnp
from jax import lax
from jax.sharding import PartitionSpec as P

TERM = 8
DMIN = 2
FINE = 4


def shifted(value, axis, steps):
    count = lax.axis_size(axis)
    first, last = (max(0, -steps), min(count, count - steps))
    return lax.ppermute(value, axis, [(source, source + steps) for source in range(first, last)])


def terminals(state, term_block):
    grouped = state.reshape(
        state.shape[0], state.shape[1], state.shape[2], state.shape[3] // TERM, TERM
    )
    target = (state.shape[0], state.shape[1], state.shape[2], term_block.shape[1], TERM)
    picked = jnp.take_along_axis(
        grouped, jnp.broadcast_to(term_block[None, :, None, :, None], target), axis=3
    )
    picked = jnp.transpose(picked, (1, 3, 0, 2, 4))
    return picked.reshape(
        picked.shape[0] * picked.shape[1], picked.shape[2], picked.shape[3] * TERM
    )


def inject(collected, source_rows, line_delay, line_live, admittance, term_block, step, state):
    reach = jnp.maximum(step + 1 - line_delay, 0).reshape(-1)
    stacked = jnp.concatenate(collected, axis=0)
    everyone = collected[0].shape[0]
    row_index = reach * everyone + source_rows
    far_values = stacked[row_index]
    far_values = far_values.reshape(
        term_block.shape[0], term_block.shape[1], state.shape[0], state.shape[2], TERM
    )
    weights = admittance * line_live.astype(jnp.float32)
    far_values = far_values * weights[:, :, None, None, None]
    blocks_here = jnp.arange(state.shape[3] // TERM, dtype=jnp.int32)
    onehot = (term_block[:, :, None] == blocks_here[None, None, :]).astype(jnp.float32)
    placed = jnp.einsum("plsct,plb->spcbt", far_values, onehot, precision=lax.Precision.HIGHEST)
    return placed.reshape(state.shape)


def advance(state, inverses, retain, sources, injected):
    driven = retain[None, :, None, :] * state + sources[None] + injected
    return jnp.einsum(
        "spcm,pnm->spcn",
        driven,
        inverses,
        precision=lax.Precision.HIGHEST,
        preferred_element_type=jnp.float32,
    )


def publish(pending, collected):
    stacked = jnp.stack(pending, axis=1)
    arrived = lax.all_gather(stacked, "sub", axis=0, tiled=True)
    return collected + [arrived[:, place] for place in range(len(pending))]


def shards(
    starts,
    inverses,
    retain,
    sources,
    coarse_decay,
    admittance,
    partner,
    line_delay,
    line_live,
    term_block,
):
    source_rows = partner.reshape(-1)
    state = starts
    collected = publish([terminals(state, term_block)], [])
    pending = []
    for step in range(FINE):
        injected = inject(
            collected, source_rows, line_delay, line_live, admittance, term_block, step, state
        )
        state = advance(state, inverses, retain, sources, injected)
        if step + 1 <= FINE - DMIN:
            pending.append(terminals(state, term_block))
            if len(pending) == DMIN or step + 1 == FINE - DMIN:
                collected = publish(pending, collected)
                pending = []
    decay = coarse_decay[:, None, :]
    offsets = state - decay[None] * starts
    combined = offsets[0]
    leading = lax.axis_index("tm") == 0
    entering = starts[0]
    for turn in range(lax.axis_size("tm") - 1):
        leaving = decay * entering + combined
        arrived = shifted(leaving, "tm", 1)
        entering = jnp.where(leading, starts[0], arrived)
    current = entering
    current = decay * current + offsets[0]
    finals = [current]
    return jnp.stack(finals)


def solution(mesh):
    return jax.shard_map(
        shards,
        mesh=mesh,
        in_specs=(
            P("tm", "sub", None, None),
            P("sub", None, None),
            P("sub", None),
            P("sub", None, None),
            P("sub", None),
            P("sub", None),
            P("sub", None),
            P("sub", None),
            P("sub", None),
            P("sub", None),
        ),
        out_specs=P("tm", "sub", None, None),
        check_vma=False,
    )
```

profile of v0, /device:TPU:0, one launch (start us, length us, event | category | flops | bytes accessed | tf_op | source)
XLA Modules:
  0.0 99.8 jit_solution(7328182231525453311)
XLA Ops:
  0.0 0.7 broadcast_add_fusion
  0.7 0.7 broadcast_compare_fusion
  1.3 0.7 fusion.43
  2.1 1.0 %copy.21 = f32[1,1,16,1024]{2,3,1,0:T(8,128)S(1)} copy(f32[1,1,16,1024]{3,2,1,0:T(8,128)} %param.12) | data formatting | bytes 131072 | tf_op args[0]
  3.2 1.0 %copy.22 = f32[1,1,16,128,8]{4,3,2,1,0:T(8,128)S(1)} copy(f32[1,1,16,128,8]{2,4,3,1,0:T(8,128)S(1)} %bitcast.260) | data formatting | bytes 131072 | tf_op jit(solution)/shard_map/reshape | solution.py:18
  4.3 9.0 %gather_fusion.4 = f32[1024]{0:T(1024)S(1)} fusion(f32[16,128,8]{2,1,0:T(8,128)S(1)} %bitcast.257, s32[1024]{0:T(1024)S(1)} %reshape.675), kind=kCustom, calls=%fused_computation.clone | custom fusion | bytes 20480 | tf_op jit(solution)/shard_map/jit(take_along_axis)/gather | solution.py:22
  13.6 10.6 %all_gather.6 = f32[64,1,1,128]{3,0,2,1:T(8,128)S(1)} all-gather(f32[8,1,1,128]{3,0,2,1:T(8,128)S(1)} %stack_reshape.9), channel_id=1, replica_groups=mesh['tm'=4,'sub'=8] {'sub'}, dimensions={0}, use_global_device_ids=true | all-gather | bytes 36864 | tf_op jit(solution)/shard_map/all_gather | solution.py:61
  24.8 0.6 gather_fusion
  27.3 5.7 %fusion.8 = f32[1,1,16,1024]{3,2,0,1:T(8,128)S(1)} fusion(f32[1,1024,1024]{2,1,0:T(8,128)} %param.13, f32[1,1,16,1024]{3,2,0,1:T(8,128)S(1)} %copy.26, f32[1,16,1024]{2,1,0:T(8,128)S(1)} %copy-done.2, f32[1,1,16,1024]{3,2,1,0:T(8,128)S(1)} %copy-done.1, f32[1024]{0:T(1024)S(1)} %bitcast.273), kind=kOutput, calls=%fused_computation.19 | convolution fusion | flops 201375744 | bytes 4460544 | tf_op jit(solution)/shard_map/spcm,pnm->spcn/dot_general | solution.py:50
  33.1 5.7 %fusion.11 = f32[1,1,16,1024]{3,2,0,1:T(8,128)S(1)} fusion(f32[1,1024,1024]{2,1,0:T(8,128)} %param.13, f32[1,1,16,1024]{3,2,0,1:T(8,128)S(1)} %copy.29, f32[1,16,1024]{2,1,0:T(8,128)S(1)} %copy-done.2, f32[1,1,16,1024]{3,2,0,1:T(8,128)S(1)} %fusion.8, f32[1024]{0:T(1024)S(1)} %bitcast.274), kind=kOutput, calls=%fused_computation.20 | convolution fusion | flops 201375744 | bytes 4460544 | tf_op jit(solution)/shard_map/spcm,pnm->spcn/dot_general | solution.py:50
  39.0 1.0 %copy.34 = f32[1,1,16,128,8]{4,3,2,1,0:T(8,128)S(1)} copy(f32[1,1,16,128,8]{2,4,3,1,0:T(8,128)S(1)} %bitcast.261) | data formatting | bytes 131072 | tf_op jit(solution)/shard_map/reshape | solution.py:18
  40.1 9.0 %gather_fusion.6 = f32[1024]{0:T(1024)S(1)} fusion(f32[16,128,8]{2,1,0:T(8,128)S(1)} %bitcast.258, s32[1024]{0:T(1024)S(1)} %reshape.675), kind=kCustom, calls=%fused_computation.2.clone | custom fusion | bytes 20480 | tf_op jit(solution)/shard_map/jit(take_along_axis)/gather | solution.py:22
  49.1 1.0 %copy.31 = f32[1,1,16,128,8]{4,3,2,1,0:T(8,128)S(1)} copy(f32[1,1,16,128,8]{2,4,3,1,0:T(8,128)S(1)} %bitcast.259) | data formatting | bytes 131072 | tf_op jit(solution)/shard_map/reshape | solution.py:18
  50.2 9.0 %gather_fusion.5 = f32[1024]{0:T(1024)S(1)} fusion(f32[16,128,8]{2,1,0:T(8,128)S(1)} %bitcast.256, s32[1024]{0:T(1024)S(1)} %reshape.675), kind=kCustom, calls=%fused_computation.1.clone | custom fusion | bytes 20480 | tf_op jit(solution)/shard_map/jit(take_along_axis)/gather | solution.py:22
  59.6 9.2 %all_gather.7 = f32[64,2,1,128]{3,0,2,1:T(8,128)S(1)} all-gather(f32[8,2,1,128]{3,0,2,1:T(8,128)S(1)} %pad_maximum_fusion), channel_id=1, replica_groups=mesh['tm'=4,'sub'=8] {'sub'}, dimensions={0}, use_global_device_ids=true | all-gather | bytes 73728 | tf_op jit(solution)/shard_map/all_gather | solution.py:61
  71.8 5.8 %fusion.38 = f32[16,1024]{1,0:T(8,128)S(1)} fusion(f32[1,1,16,1024]{3,2,0,1:T(8,128)S(1)} %copy.41, f32[1,1024,1024]{2,1,0:T(8,128)} %param.13, f32[1,16,1024]{2,1,0:T(8,128)S(1)} %copy-done.2, f32[1,1,16,1024]{3,2,0,1:T(8,128)S(1)} %copy.38, f32[1,1,16,1024]{3,2,0,1:T(8,128)S(1)} %fusion.11, f32[1024]{0:T(1024)S(1)} %bitcast.275), kind=kOutput, calls=%fused_computation.29 | convolution fusion | flops 201424896 | bytes 4526080 | tf_op jit(solution)/shard_map/spcm,pnm->spcn/dot_general | solution.py:50
  77.7 3.6 %fusion.53 = (f32[1,16,1024]{2,1,0:T(8,128)S(1)}, f32[1,16,1024]{2,1,0:T(8,128)S(1)}) fusion(f32[1,1,16,1024]{3,2,1,0:T(8,128)S(1)} %copy-done.1, f32[1024]{0:T(1024)S(1)} %bitcast.269, f32[16,1024]{1,0:T(8,128)S(1)} %fusion.38, f32[1,1024,1024]{2,1,0:T(8,128)S(1)} %copy-done), kind=kOutput, calls=%fused_computation.52 | convolution fusion | flops 201392128 | bytes 4460544 | tf_op jit(solution)/shard_map/spcm,pnm->spcn/dot_general | solution.py:50
  81.3 3.5 %collective-permute-start = (f32[1,16,1024]{2,1,0:T(8,128)S(1)}, f32[1,16,1024]{2,1,0:T(8,128)S(1)}, u32[]{:S(2)}, u32[]{:S(2)}) collective-permute-start(f32[1,16,1024]{2,1,0:T(8,128)S(1)} %get-tuple-element.18), channel_id=1, source_target_pairs={{0,8},{8,16},{16,24},{1,9},{9,17},{17,25},{2,10},{10,18},{18,26},{... | collective-permute-start | bytes 196616 | tf_op jit(solution)/shard_map/ppermute | solution.py:14
  84.8 1.9 %collective-permute-done = f32[1,16,1024]{2,1,0:T(8,128)S(1)} collective-permute-done((f32[1,16,1024]{2,1,0:T(8,128)S(1)}, f32[1,16,1024]{2,1,0:T(8,128)S(1)}, u32[]{:S(2)}, u32[]{:S(2)}) %collective-permute-start) | collective-permute-done | bytes 65568 | tf_op jit(solution)/shard_map/ppermute | solution.py:14
  86.7 4.4 %collective-permute-start.1 = (f32[1,16,1024]{2,1,0:T(8,128)S(1)}, f32[1,16,1024]{2,1,0:T(8,128)S(1)}, u32[]{:S(2)}, u32[]{:S(2)}) collective-permute-start(f32[1,16,1024]{2,1,0:T(8,128)S(1)} %fusion.55), channel_id=1, source_target_pairs={{0,8},{8,16},{16,24},{1,9},{9,17},{17,25},{2,10},{10,18},{18,26},{... | collective-permute-start | bytes 196616 | tf_op jit(solution)/shard_map/ppermute | solution.py:14
  91.0 1.9 %collective-permute-done.1 = f32[1,16,1024]{2,1,0:T(8,128)S(1)} collective-permute-done((f32[1,16,1024]{2,1,0:T(8,128)S(1)}, f32[1,16,1024]{2,1,0:T(8,128)S(1)}, u32[]{:S(2)}, u32[]{:S(2)}) %collective-permute-start.1) | collective-permute-done | bytes 65568 | tf_op jit(solution)/shard_map/ppermute | solution.py:14
  93.0 4.3 %collective-permute-start.2 = (f32[1,16,1024]{2,1,0:T(8,128)S(1)}, f32[1,16,1024]{2,1,0:T(8,128)S(1)}, u32[]{:S(2)}, u32[]{:S(2)}) collective-permute-start(f32[1,16,1024]{2,1,0:T(8,128)S(1)} %fusion.57), channel_id=1, source_target_pairs={{0,8},{8,16},{16,24},{1,9},{9,17},{17,25},{2,10},{10,18},{18,26},{... | collective-permute-start | bytes 196616 | tf_op jit(solution)/shard_map/ppermute | solution.py:14
  97.2 1.9 %collective-permute-done.2 = f32[1,16,1024]{2,1,0:T(8,128)S(1)} collective-permute-done((f32[1,16,1024]{2,1,0:T(8,128)S(1)}, f32[1,16,1024]{2,1,0:T(8,128)S(1)}, u32[]{:S(2)}, u32[]{:S(2)}) %collective-permute-start.2) | collective-permute-done | bytes 65568 | tf_op jit(solution)/shard_map/ppermute | solution.py:14
  99.1 0.6 fusion.60
  (68 shorter events, 6.6 us)
Async XLA Ops:
  4.2 9.2 %copy-start.5 = (s32[1,8]{1,0:T(1,128)S(1)}, s32[1,8]{1,0:T(1,128)}, u32[]{:S(2)}) copy-start(s32[1,8]{1,0:T(1,128)} %param.21) | copy-start | bytes 100
  4.2 20.0 %copy-start.6 = (s32[1,8]{1,0:T(1,128)S(1)}, s32[1,8]{1,0:T(1,128)}, u32[]{:S(2)}) copy-start(s32[1,8]{1,0:T(1,128)} %param.18) | copy-start | bytes 100
  4.2 20.0 %copy-start.7 = (s32[1,8]{1,0:T(1,128)S(1)}, s32[1,8]{1,0:T(1,128)}, u32[]{:S(2)}) copy-start(s32[1,8]{1,0:T(1,128)} %param.19) | copy-start | bytes 100
  4.3 21.1 %copy-start.8 = (f32[1,8]{1,0:T(1,128)S(1)}, f32[1,8]{1,0:T(1,128)}, u32[]{:S(2)}) copy-start(f32[1,8]{1,0:T(1,128)} %param.17) | copy-start | bytes 100
  4.3 21.1 %copy-start.9 = (s32[1,8]{1,0:T(1,128)S(1)}, s32[1,8]{1,0:T(1,128)}, u32[]{:S(2)}) copy-start(s32[1,8]{1,0:T(1,128)} %param.20) | copy-start | bytes 100
  4.3 23.0 %copy-start.1 = (f32[1,1,16,1024]{3,2,1,0:T(8,128)S(1)}, f32[1,1,16,1024]{3,2,1,0:T(8,128)}, u32[]{:S(2)}) copy-start(f32[1,1,16,1024]{3,2,1,0:T(8,128)} %param.12) | copy-start | bytes 196612
  4.3 22.9 %copy-start.2 = (f32[1,16,1024]{2,1,0:T(8,128)S(1)}, f32[1,16,1024]{2,1,0:T(8,128)}, u32[]{:S(2)}) copy-start(f32[1,16,1024]{2,1,0:T(8,128)} %param.15) | copy-start | bytes 196612
  4.3 22.9 %copy-start.4 = (f32[1,1024]{1,0:T(1,128)S(1)}, f32[1,1024]{1,0:T(1,128)}, u32[]{:S(2)}) copy-start(f32[1,1024]{1,0:T(1,128)} %param.14) | copy-start | bytes 12292
  59.4 18.3 %copy-start.3 = (f32[1,1024]{1,0:T(1,128)S(1)}, f32[1,1024]{1,0:T(1,128)}, u32[]{:S(2)}) copy-start(f32[1,1024]{1,0:T(1,128)} %param.16) | copy-start | bytes 12292
  71.8 5.9 %copy-start = (f32[1,1024,1024]{2,1,0:T(8,128)S(1)}, f32[1,1024,1024]{2,1,0:T(8,128)}, u32[]{:S(2)}) copy-start(f32[1,1024,1024]{2,1,0:T(8,128)} %param.13) | copy-start | bytes 12582916
  81.3 5.4 %collective-permute-start = (f32[1,16,1024]{2,1,0:T(8,128)S(1)}, f32[1,16,1024]{2,1,0:T(8,128)S(1)}, u32[]{:S(2)}, u32[]{:S(2)}) collective-permute-start(f32[1,16,1024]{2,1,0:T(8,128)S(1)} %get-tuple-element.18), channel_id=1, source_target_pairs={{0,8},{8,16},{16,24},{1,9},{9,17},{17,25},{2,10},{10,18},{18,26},{... | collective-permute-start | bytes 196616 | tf_op jit(solution)/shard_map/ppermute | solution.py:14
  86.7 6.2 %collective-permute-start.1 = (f32[1,16,1024]{2,1,0:T(8,128)S(1)}, f32[1,16,1024]{2,1,0:T(8,128)S(1)}, u32[]{:S(2)}, u32[]{:S(2)}) collective-permute-start(f32[1,16,1024]{2,1,0:T(8,128)S(1)} %fusion.55), channel_id=1, source_target_pairs={{0,8},{8,16},{16,24},{1,9},{9,17},{17,25},{2,10},{10,18},{18,26},{... | collective-permute-start | bytes 196616 | tf_op jit(solution)/shard_map/ppermute | solution.py:14
  93.0 6.2 %collective-permute-start.2 = (f32[1,16,1024]{2,1,0:T(8,128)S(1)}, f32[1,16,1024]{2,1,0:T(8,128)S(1)}, u32[]{:S(2)}, u32[]{:S(2)}) collective-permute-start(f32[1,16,1024]{2,1,0:T(8,128)S(1)} %fusion.57), channel_id=1, source_target_pairs={{0,8},{8,16},{16,24},{1,9},{9,17},{17,25},{2,10},{10,18},{18,26},{... | collective-permute-start | bytes 196616 | tf_op jit(solution)/shard_map/ppermute | solution.py:14
where the time goes:
time: 100 us; the launch traced here: 99.8 us
  local copies, waits for them, and re-layouts  36.7 us (37%)
  matrix products  21.9 us (22%)
  blocking collectives  19.8 us (20%)
  starting transfers between devices  12.1 us (12%)
  waiting for transfers between devices  5.65 us (6%)
  other arithmetic  3.07 us (3%)
    gather x7, local copies, waits for them, and re-layouts, terminals(): jnp.take_along_axis(grouped, jnp.broadcast_to(term_block[None, :, None, :...  27.3 us
    dot_general x4, matrix products, advance(): jnp.einsum('spcm,pnm->spcn', driven, inverses, precision=lax.Precision.HI...  20.8 us
    all_gather x2, blocking collectives, publish(): arrived = lax.all_gather(stacked, 'sub', axis=0, tiled=True)  19.8 us
    ppermute x3, starting transfers between devices, shifted(): lax.ppermute(value, axis, [(source, source + steps) for source in range(f...  12.1 us
    ppermute x3, waiting for transfers between devices, shifted(): lax.ppermute(value, axis, [(source, source + steps) for source in range(f...  5.65 us
    reshape x3, local copies, waits for them, and re-layouts, terminals(): state.reshape(state.shape[0], state.shape[1], state.shape[2], state.shape...  3.06 us
    gather x4, local copies, waits for them, and re-layouts, inject(): far_values = stacked[row_index]  2.22 us
  transfers between devices with their start and end apart: 3, of which 3 were waited for; matrix products, arithmetic and copies ran while one was open for 0% of the time, Pallas kernels for 0%

commit v1 on v0

v1 whole, which is shorter than its diff:
```python
import functools

import jax
import jax.numpy as jnp
from jax import lax
from jax.experimental import pallas as pl
from jax.experimental.pallas import tpu as pltpu
from jax.sharding import PartitionSpec as P

TERM = 8
CHUNKS = 4

f32 = jnp.float32
bf16 = jnp.bfloat16
ROWS_BY_ROWS = (((1,), (1,)), ((), ()))


def split(value):
    high = value.astype(bf16)
    return high, (value - high.astype(f32)).astype(bf16)


def stacked(value):
    return jnp.concatenate(split(value), axis=0)


def folded(value):
    half = value.shape[0] // 2
    return value[:half] + value[half:]


def times_rows(left, high, low):
    return lax.dot_general(left, high, ROWS_BY_ROWS, preferred_element_type=f32) + lax.dot_general(
        left, low, ROWS_BY_ROWS, preferred_element_type=f32
    )


def times(left, right):
    return jnp.dot(left, right, preferred_element_type=f32)


def slot_lanes(lines, width, read):
    slot = lax.broadcasted_iota(jnp.int32, (1, width), 1) // TERM % lines
    row = jnp.full((1, width), read(0))
    for line in range(1, lines):
        row = jnp.where(slot == line, read(line), row)
    return row


def first_kernel(
    block_ref, partner_ref, live_ref, admittance_ref,
    start_ref, source_ref, retain_ref, inverse_ref,
    package_ref, moved_ref, high_ref, low_ref,
    held, picked, arrived,
):
    cols, nodes = start_ref.shape
    lines = block_ref.shape[1]
    points = lines * TERM
    depth = nodes // CHUNKS
    copies = []
    for part in range(CHUNKS):
        rows = pl.ds(part * depth, depth)
        copies.append(
            pltpu.make_async_copy(inverse_ref.at[rows], held.at[rows], arrived.at[part])
        )
        copies[-1].start()
    offset = lax.broadcasted_iota(jnp.int32, (TERM, nodes), 1) - lax.broadcasted_iota(
        jnp.int32, (TERM, nodes), 0
    )
    chosen = jnp.concatenate(
        [(offset == block_ref[0, line] * TERM).astype(f32) for line in range(lines)], axis=0
    ).astype(bf16)
    retain = retain_ref[...]
    source = source_ref[...]
    start = start_ref[...]
    left = jnp.concatenate([stacked(retain * start + source), chosen], axis=0)
    for part in range(CHUNKS):
        copies[part].wait()
        rows = pl.ds(part * depth, depth)
        high, low = split(held[rows, :])
        high_ref[rows, :] = high
        low_ref[rows, :] = low
        out = times_rows(left, high, low)
        moved_ref[:cols, rows] = folded(out[: 2 * cols])
        moved_ref[cols:, rows] = out[2 * cols :]
    picked[:points, :] = jnp.zeros((points, nodes), f32)
    for line in range(lines):
        picked[points + line * TERM : points + (line + 1) * TERM, :] = held[
            pl.ds(pl.multiple_of(block_ref[0, line] * TERM, TERM), TERM), :
        ]
    moved = moved_ref[...]
    driven = jnp.concatenate(
        [retain * moved[:cols] + source, retain * moved[cols:]], axis=0
    )
    second = folded(times_rows(stacked(driven), *split(picked[...])))
    everything = jnp.concatenate([start, moved], axis=0)
    twice = jnp.concatenate([chosen, chosen], axis=0)
    firsts = folded(
        lax.dot_general(stacked(everything), twice, ROWS_BY_ROWS, preferred_element_type=f32)
    )
    lane = lax.broadcasted_iota(jnp.int32, (cols, 2 * points), 1)
    table = slot_lanes(lines, 2 * points, lambda line: partner_ref[0, line] * TERM)
    table = (table + lax.broadcasted_iota(jnp.int32, table.shape, 1) % TERM).astype(f32)
    package_ref[:cols, :] = jnp.where(lane < points, firsts[:cols], table)
    package_ref[cols : 2 * cols, :] = jnp.where(
        lane < points, firsts[cols : 2 * cols], second[:cols]
    )
    answers = firsts[2 * cols :] + second[cols:]
    for line in range(lines):
        weight = admittance_ref[0, line] * live_ref[0, line].astype(f32)
        rows = slice(line * TERM, (line + 1) * TERM)
        package_ref[2 * cols + line * TERM : 2 * cols + (line + 1) * TERM, :] = (
            weight * answers[rows]
        )


def middle_kernel(
    moved_ref, high_ref, low_ref, start_ref, source_ref, retain_ref, decay_ref,
    base_ref, reply_high_ref, reply_low_ref,
):
    cols, nodes = start_ref.shape
    points = moved_ref.shape[0] - cols
    retain = retain_ref[...]
    source = source_ref[...]
    state = moved_ref[...]
    replies = [state[cols:]]
    for _ in range(3):
        driven = jnp.concatenate(
            [retain * state[:cols] + source, retain * state[cols:]], axis=0
        )
        state = folded(times_rows(stacked(driven), high_ref[...], low_ref[...]))
        replies.append(state[cols:])
    kept = decay_ref[...] * start_ref[...]
    offset = state[:cols] - kept
    leading = lax.axis_index("tm") == 0
    base_ref[...] = jnp.where(leading, offset + kept, offset)
    reply = jnp.concatenate(
        [replies[3] + replies[2], jnp.zeros((points, nodes), f32), replies[1], replies[0]], axis=0
    )
    reply_high_ref[...], reply_low_ref[...] = split(reply)


def last_kernel(
    count, partner_ref, delay_ref, live_ref, admittance_ref, here_ref, there_ref, base_ref,
    reply_high_ref, reply_low_ref, out_ref,
):
    cols = base_ref.shape[0]
    lines = partner_ref.shape[1]
    points = lines * TERM
    width = 2 * points
    mine = lax.axis_index("sub")
    lane = lax.broadcasted_iota(jnp.int32, (cols, width), 1)
    pairs = []
    tables = []
    for pair in range(count // 2):
        even = here_ref[pair, :cols, :]
        odd = pltpu.roll(there_ref[pair, :cols, :], points, 1)
        pairs.append(jnp.where(lane < points, even, odd))
        tables.append(
            jnp.where(lane < points, pltpu.roll(even, points, 1), pltpu.roll(odd, points, 1))[:1]
        )
    snapshot = jnp.concatenate(pairs, axis=1)
    table = jnp.concatenate(tables, axis=1).astype(jnp.int32) ^ (mine * points)
    total = count * points
    route = (lax.broadcasted_iota(jnp.int32, (total, total), 0) == table).astype(f32).astype(bf16)
    far = folded(times(stacked(snapshot), route))
    later = []
    for pair in range(count // 2):
        both = far[:, pair * width : (pair + 1) * width]
        rows = jnp.concatenate(
            [stacked(jnp.where(lane < points, both, 0.0)), stacked(jnp.where(lane < points, 0.0, both))],
            axis=0,
        )
        answers = jnp.concatenate(
            [here_ref[pair, 2 * cols :, :], there_ref[pair, 2 * cols :, :]], axis=0
        )
        high, low = split(answers)
        sums = times(rows, high) + times(rows, low)
        later.append(here_ref[pair, cols : 2 * cols, :] + folded(sums[: 2 * cols]))
        later.append(there_ref[pair, cols : 2 * cols, :] + folded(sums[2 * cols :]))
    known = jnp.concatenate(later + [snapshot], axis=1)
    delay = slot_lanes(lines, width, lambda line: delay_ref[0, line])
    slot = slot_lanes(lines, width, lambda line: partner_ref[0, line])
    weight = slot_lanes(
        lines, width, lambda line: admittance_ref[0, line] * live_ref[0, line].astype(f32)
    )
    index = lax.broadcasted_iota(jnp.int32, (1, width), 1)
    source = (slot * TERM + index % TERM) ^ (mine * points)
    late = index >= points
    within = source % points
    start = source // points * width + within
    wanted = jnp.where(
        late,
        jnp.where(delay == 2, start + points, jnp.where(delay == 3, start, count * width + source)),
        jnp.where(delay == 2, start, count * width + source),
    )
    pick = (lax.broadcasted_iota(jnp.int32, (known.shape[1], width), 0) == wanted)
    chosen = folded(times(stacked(known), pick.astype(f32).astype(bf16)))
    first = jnp.where(lane < points, far[:, :width], 0.0)
    rows = stacked(jnp.concatenate([weight * first, weight * chosen], axis=1))
    out_ref[...] = base_ref[...] + folded(
        times(rows, reply_high_ref[...]) + times(rows, reply_low_ref[...])
    )


def combine_kernel(count, decay_ref, *refs):
    parts, out_ref = refs[:count], refs[count]
    mine = lax.axis_index("tm")
    decay = decay_ref[...]
    loaded = [part[...] for part in parts]
    total = jnp.zeros_like(loaded[0])
    for turn in range(count):
        value = loaded[0]
        for place in range(1, count):
            value = jnp.where((mine ^ turn) == place, loaded[place], value)
        total = jnp.where(turn <= mine, decay * total + value, total)
    out_ref[...] = total


def exchanged(value, axis, count, flip):
    return lax.ppermute(value, axis, [(source, source ^ flip) for source in range(count)])


VMEM = pl.BlockSpec(memory_space=pltpu.VMEM)
SMEM = pl.BlockSpec(memory_space=pltpu.SMEM)
ANY = pl.BlockSpec(memory_space=pl.ANY)


def shards(
    times_count, subs, starts, inverses, retain, sources, coarse_decay, admittance, partner,
    line_delay, line_live, term_block,
):
    cols, nodes = starts.shape[2:]
    points = partner.shape[1] * TERM
    width = 2 * points
    start = starts.reshape(cols, nodes)
    source = sources.reshape(cols, nodes)
    inverse = inverses.reshape(nodes, nodes)
    shape = jax.ShapeDtypeStruct
    package, moved, high, low = pl.pallas_call(
        first_kernel,
        out_shape=(
            shape((2 * cols + points, width), f32),
            shape((cols + points, nodes), f32),
            shape((nodes, nodes), bf16),
            shape((nodes, nodes), bf16),
        ),
        in_specs=[SMEM] * 4 + [VMEM] * 3 + [ANY],
        out_specs=(VMEM,) * 4,
        scratch_shapes=[
            pltpu.VMEM((nodes, nodes), f32),
            pltpu.VMEM((width, nodes), f32),
            pltpu.SemaphoreType.DMA((CHUNKS,)),
        ],
        compiler_params=pltpu.CompilerParams(vmem_limit_bytes=24 << 20),
        name="first",
    )(term_block, partner, line_live, admittance, start, source, retain, inverse)

    base, reply_high, reply_low = pl.pallas_call(
        middle_kernel,
        out_shape=(
            shape((cols, nodes), f32),
            shape((4 * points, nodes), bf16),
            shape((4 * points, nodes), bf16),
        ),
        in_specs=[VMEM] * 7,
        out_specs=(VMEM,) * 3,
        compiler_params=pltpu.CompilerParams(vmem_limit_bytes=24 << 20),
        name="middle",
    )(moved, high, low, start, source, retain, coarse_decay)

    here = jnp.stack(
        [package] + [exchanged(package, "sub", subs, flip) for flip in range(2, subs, 2)]
    )
    there = exchanged(here, "sub", subs, 1)

    value = pl.pallas_call(
        functools.partial(last_kernel, subs),
        out_shape=shape((cols, nodes), f32),
        in_specs=[SMEM] * 4 + [VMEM] * 5,
        out_specs=VMEM,
        compiler_params=pltpu.CompilerParams(vmem_limit_bytes=40 << 20),
        name="last",
    )(partner, line_delay, line_live, admittance, here, there, base, reply_high, reply_low)

    parts = [value] + [
        exchanged(value, "tm", times_count, flip) for flip in range(1, times_count)
    ]
    ends = pl.pallas_call(
        functools.partial(combine_kernel, times_count),
        out_shape=shape((cols, nodes), f32),
        in_specs=[VMEM] * (1 + times_count),
        out_specs=VMEM,
        compiler_params=pltpu.CompilerParams(vmem_limit_bytes=8 << 20),
        name="combine",
    )(coarse_decay, *parts)
    return ends.reshape(starts.shape)


def solution(mesh):
    return jax.shard_map(
        functools.partial(shards, mesh.shape["tm"], mesh.shape["sub"]),
        mesh=mesh,
        in_specs=(
            P("tm", "sub", None, None),
            P("sub", None, None),
            P("sub", None),
            P("sub", None, None),
            P("sub", None),
            P("sub", None),
            P("sub", None),
            P("sub", None),
            P("sub", None),
            P("sub", None),
        ),
        out_specs=P("tm", "sub", None, None),
        check_vma=False,
    )
```

time: 100 us -> 36.5 us (0.36)
  local copies, waits for them, and re-layouts: 36.7 us -> 7.21 us
  matrix products: 21.9 us -> 0 us
  blocking collectives: 19.8 us -> 0 us
  Pallas kernels: 0 us -> 10.4 us
  waiting for transfers between devices: 5.65 us -> 9.26 us
  other arithmetic: 3.07 us -> 0.01 us
  starting transfers between devices: 12.1 us -> 9.11 us
    gather x11 -> x0, local copies, waits for them, and re-layouts: 29.5 us -> none  [the longest x7 27.3 us: terminals(): jnp.take_along_axis(grouped, jnp.broadcast_to(term_block[None, :, None, :...]
    dot_general x8 -> x0, matrix products: 21.9 us -> none  [the longest x4 20.8 us: advance(): jnp.einsum('spcm,pnm->spcn', driven, inverses, precision=lax.Precision.HI...]
    all_gather x2 -> x0, blocking collectives: 19.8 us -> none  [publish(): arrived = lax.all_gather(stacked, 'sub', axis=0, tiled=True)]
    pallas_call x0 -> x4, Pallas kernels: none -> 10.4 us  [the longest x1 4.27 us: shards(): pl.pallas_call(middle_kernel, out_shape=(shape((cols, nodes), f32), shape...]
    unnamed x21 -> x30, local copies, waits for them, and re-layouts: 1.1 us -> 7.21 us
    reshape x7 -> x0, local copies, waits for them, and re-layouts: 3.71 us -> none  [the longest x3 3.06 us: terminals(): state.reshape(state.shape[0], state.shape[1], state.shape[2], state.shape...]
    ppermute x3 -> x7, waiting for transfers between devices: 5.65 us -> 9.26 us  [exchanged(): lax.ppermute(value, axis, [(source, source ^ flip) for source in range(co...]
    ppermute x3 -> x7, starting transfers between devices: 12.1 us -> 9.11 us  [exchanged(): lax.ppermute(value, axis, [(source, source ^ flip) for source in range(co...]
  transfers between devices with their start and end apart: 3 -> 7, of which waited for: 3 -> 5; matrix products, arithmetic and copies ran while one was open for 0% -> 0% of each run, Pallas kernels for 0% -> 12%
where the time goes in v1:
time: 36.5 us; the launch traced here: 36.2 us
  Pallas kernels  10.4 us (28%)
  waiting for transfers between devices  9.26 us (25%)
  starting transfers between devices  9.11 us (25%)
  local copies, waits for them, and re-layouts  7.21 us (20%)
    ppermute x7, waiting for transfers between devices, exchanged(): lax.ppermute(value, axis, [(source, source ^ flip) for source in range(co...  9.26 us
    ppermute x7, starting transfers between devices, exchanged(): lax.ppermute(value, axis, [(source, source ^ flip) for source in range(co...  9.11 us
    unnamed x30, local copies, waits for them, and re-layouts  7.21 us
    pallas_call x1, Pallas kernels, shards(): pl.pallas_call(middle_kernel, out_shape=(shape((cols, nodes), f32), shape...  4.27 us
    pallas_call x1, Pallas kernels, shards(): pl.pallas_call(first_kernel, out_shape=(shape((2 * cols + points, width),...  3.98 us
    pallas_call x1, Pallas kernels, shards(): pl.pallas_call(functools.partial(last_kernel, subs), out_shape=shape((col...  1.49 us
  transfers between devices with their start and end apart: 7, of which 5 were waited for; matrix products, arithmetic and copies ran while one was open for 0% of the time, Pallas kernels for 12%

profile of v1, /device:TPU:0, one launch (start us, length us, event | category | flops | bytes accessed | tf_op | source)
XLA Modules:
  0.0 36.2 jit_solution(8945904160954532760)
XLA Ops:
  0.0 2.2 %copy-done = f32[1,1024,1024]{2,1,0:T(8,128)S(1)} copy-done((f32[1,1024,1024]{2,1,0:T(8,128)S(1)}, f32[1,1024,1024]{2,1,0:T(8,128)}, u32[]{:S(2)}) %copy-start) | copy-done | bytes 4194328
  2.2 0.8 %copy-done.1 = f32[1,1,16,1024]{3,2,1,0:T(8,128)S(1)} copy-done((f32[1,1,16,1024]{3,2,1,0:T(8,128)S(1)}, f32[1,1,16,1024]{3,2,1,0:T(8,128)}, u32[]{:S(2)}) %copy-start.1) | copy-done | bytes 65560
  3.0 0.8 %copy-done.3 = f32[1,16,1024]{2,1,0:T(8,128)S(1)} copy-done((f32[1,16,1024]{2,1,0:T(8,128)S(1)}, f32[1,16,1024]{2,1,0:T(8,128)}, u32[]{:S(2)}) %copy-start.3) | copy-done | bytes 65560
  3.9 0.7 %copy-done.5 = f32[1,1024]{1,0:T(1,128)S(1)} copy-done((f32[1,1024]{1,0:T(1,128)S(1)}, f32[1,1024]{1,0:T(1,128)}, u32[]{:S(2)}) %copy-start.5) | copy-done | bytes 4120
  4.6 0.7 %copy-done.7 = s32[1,8]{1,0:T(1,128)S(1)} copy-done((s32[1,8]{1,0:T(1,128)S(1)}, s32[1,8]{1,0:T(1,128)}, u32[]{:S(2)}) %copy-start.7) | copy-done | bytes 56
  5.2 0.7 %copy-done.9 = s32[1,8]{1,0:T(1,128)S(1)} copy-done((s32[1,8]{1,0:T(1,128)S(1)}, s32[1,8]{1,0:T(1,128)}, u32[]{:S(2)}) %copy-start.9) | copy-done | bytes 56
  5.9 0.7 %copy-done.11 = f32[1,8]{1,0:T(1,128)S(1)} copy-done((f32[1,8]{1,0:T(1,128)S(1)}, f32[1,8]{1,0:T(1,128)}, u32[]{:S(2)}) %copy-start.11) | copy-done | bytes 56
  6.5 0.7 %copy-done.13 = s32[1,8]{1,0:T(1,128)S(1)} copy-done((s32[1,8]{1,0:T(1,128)S(1)}, s32[1,8]{1,0:T(1,128)}, u32[]{:S(2)}) %copy-start.13) | copy-done | bytes 56
  7.2 4.0 %first.1 = (f32[96,128]{1,0:T(8,128)S(1)}, f32[80,1024]{1,0:T(8,128)S(1)}, bf16[1024,1024]{1,0:T(8,128)(2,1)S(1)}, bf16[1024,1024]{1,0:T(8,128)(2,1)S(1)}) custom-call(s32[1,8]{1,0:T(1,128)S(1)} %copy-done.13, s32[1,8]{1,0:T(1,128)S(1)} %copy-done.7, s32[1,8]{1,0:T(1,128)S(1)} %copy-done.9, f32[1,8]{1,0:T(1,128)S(1)} %copy-done.11, f32[16,1024]{1,0:T(8,128)S(1)} %bitcast.9, ...), custom_call_target="tpu_custom_call" | custom-call | tf_op jit(solution)/shard_map/first/pallas_call | solution.py:240
  11.2 4.0 %collective-permute-start.2 = (f32[96,128]{1,0:T(8,128)S(1)}, f32[96,128]{1,0:T(8,128)S(1)}, u32[]{:S(2)}, u32[]{:S(2)}) collective-permute-start(f32[96,128]{1,0:T(8,128)S(1)} %get-tuple-element.12), channel_id=1, source_target_pairs={{0,6},{1,7},{2,4},{3,5},{4,2},{5,3},{6,0},{7,1},{8,14},{9,15},{10,... | collective-permute-start | bytes 147464 | tf_op jit(solution)/shard_map/ppermute | solution.py:221
  15.2 0.5 %collective-permute-start.1 = (f32[96,128]{1,0:T(8,128)S(1)}, f32[96,128]{1,0:T(8,128)S(1)}, u32[]{:S(2)}, u32[]{:S(2)}) collective-permute-start(f32[96,128]{1,0:T(8,128)S(1)} %get-tuple-element.12), channel_id=1, source_target_pairs={{0,4},{1,5},{2,6},{3,7},{4,0},{5,1},{6,2},{7,3},{8,12},{9,13},{10,... | collective-permute-start | bytes 147464 | tf_op jit(solution)/shard_map/ppermute | solution.py:221
  15.7 0.1 collective-permute-start
  15.8 1.4 %collective-permute-done.2 = f32[96,128]{1,0:T(8,128)S(1)} collective-permute-done((f32[96,128]{1,0:T(8,128)S(1)}, f32[96,128]{1,0:T(8,128)S(1)}, u32[]{:S(2)}, u32[]{:S(2)}) %collective-permute-start.2) | collective-permute-done | bytes 49184 | tf_op jit(solution)/shard_map/ppermute | solution.py:221
  17.2 2.0 %collective-permute-done.1 = f32[96,128]{1,0:T(8,128)S(1)} collective-permute-done((f32[96,128]{1,0:T(8,128)S(1)}, f32[96,128]{1,0:T(8,128)S(1)}, u32[]{:S(2)}, u32[]{:S(2)}) %collective-permute-start.1) | collective-permute-done | bytes 49184 | tf_op jit(solution)/shard_map/ppermute | solution.py:221
  19.3 0.5 %collective-permute-done = f32[96,128]{1,0:T(8,128)S(1)} collective-permute-done((f32[96,128]{1,0:T(8,128)S(1)}, f32[96,128]{1,0:T(8,128)S(1)}, u32[]{:S(2)}, u32[]{:S(2)}) %collective-permute-start) | collective-permute-done | bytes 49184 | tf_op jit(solution)/shard_map/ppermute | solution.py:221
  19.8 0.1 collective-permute-start.3
  19.9 0.0 copy-start.8
  19.9 4.3 %middle.1 = (f32[16,1024]{1,0:T(8,128)S(1)}, bf16[256,1024]{1,0:T(8,128)(2,1)S(1)}, bf16[256,1024]{1,0:T(8,128)(2,1)S(1)}) custom-call(f32[80,1024]{1,0:T(8,128)S(1)} %get-tuple-element.13.moved_ref, bf16[1024,1024]{1,0:T(8,128)(2,1)S(1)} %get-tuple-element.14.high_ref, bf16[1024,1024]{1,0:T(8,128)(2,1)S(1)} %get-tuple-element.15.low_ref, ...), custom_call_target="tpu_custom_call" | custom-call | tf_op jit(solution)/shard_map/middle/pallas_call | solution.py:259
  24.3 1.5 %last.1.refs_0_ = f32[16,1024]{1,0:T(8,128)S(1)} custom-call(s32[1,8]{1,0:T(1,128)S(1)} %copy-done.8, s32[1,8]{1,0:T(1,128)S(1)} %copy-done.14, s32[1,8]{1,0:T(1,128)S(1)} %copy-done.10, f32[1,8]{1,0:T(1,128)S(1)} %copy-done.12, f32[4,96,128]{2,1,0:T(8,128)S(1)} %pad_maximum_fusion.here_ref, f32[4,96,128]{2,1,0:T(8,128)S(1)} %collective-permute-done.3.there_ref, ...), custom_call_target="tpu_custom_call" | custom-call | tf_op jit(solution)/shard_map/last/pallas_call | solution.py:277
  25.7 3.6 %collective-permute-start.6 = (f32[16,1024]{1,0:T(8,128)S(1)}, f32[16,1024]{1,0:T(8,128)S(1)}, u32[]{:S(2)}, u32[]{:S(2)}) collective-permute-start(f32[16,1024]{1,0:T(8,128)S(1)} %last.1.refs_0_), channel_id=1, source_target_pairs={{0,24},{8,16},{16,8},{24,0},{1,25},{9,17},{17,9},{25,1},{2,26},{10... | collective-permute-start | bytes 196616 | tf_op jit(solution)/shard_map/ppermute | solution.py:221
  29.4 0.8 %collective-permute-start.4 = (f32[16,1024]{1,0:T(8,128)S(1)}, f32[16,1024]{1,0:T(8,128)S(1)}, u32[]{:S(2)}, u32[]{:S(2)}) collective-permute-start(f32[16,1024]{1,0:T(8,128)S(1)} %last.1.refs_0_), channel_id=1, source_target_pairs={{0,8},{8,0},{16,24},{24,16},{1,9},{9,1},{17,25},{25,17},{2,10},{10... | collective-permute-start | bytes 196616 | tf_op jit(solution)/shard_map/ppermute | solution.py:221
  30.2 2.2 %collective-permute-done.6.refs_3_ = f32[16,1024]{1,0:T(8,128)S(1)} collective-permute-done((f32[16,1024]{1,0:T(8,128)S(1)}, f32[16,1024]{1,0:T(8,128)S(1)}, u32[]{:S(2)}, u32[]{:S(2)}) %collective-permute-start.6) | collective-permute-done | bytes 65568 | tf_op jit(solution)/shard_map/ppermute | solution.py:221
  32.3 3.1 %collective-permute-done.5.refs_2_ = f32[16,1024]{1,0:T(8,128)S(1)} collective-permute-done((f32[16,1024]{1,0:T(8,128)S(1)}, f32[16,1024]{1,0:T(8,128)S(1)}, u32[]{:S(2)}, u32[]{:S(2)}) %collective-permute-start.5) | collective-permute-done | bytes 65568 | tf_op jit(solution)/shard_map/ppermute | solution.py:221
  35.5 0.7 %combine.1 = f32[16,1024]{1,0:T(8,128)} custom-call(f32[1,1024]{1,0:T(1,128)S(1)} %copy-done.6, f32[16,1024]{1,0:T(8,128)S(1)} %last.1.refs_0_, f32[16,1024]{1,0:T(8,128)S(1)} %collective-permute-done.4.refs_1_, f32[16,1024]{1,0:T(8,128)S(1)} %collective-permute-done.5.refs_2_, f32[16,1024]{1,0:T(8,128)S(1)} %collective-permute-done.6.refs_3_), custom_call_target="tpu_custom_call" | custom-call | tf_op jit(solution)/shard_map/combine/pallas_call | solution.py:289
  (25 shorter events, 0.1 us)
Async XLA Ops:
  0.0 2.2 %copy-start = (f32[1,1024,1024]{2,1,0:T(8,128)S(1)}, f32[1,1024,1024]{2,1,0:T(8,128)}, u32[]{:S(2)}) copy-start(f32[1,1024,1024]{2,1,0:T(8,128)} %param.11) | copy-start | bytes 12582916
  2.2 0.8 %copy-start.1 = (f32[1,1,16,1024]{3,2,1,0:T(8,128)S(1)}, f32[1,1,16,1024]{3,2,1,0:T(8,128)}, u32[]{:S(2)}) copy-start(f32[1,1,16,1024]{3,2,1,0:T(8,128)} %param.10) | copy-start | bytes 196612
  3.0 0.8 %copy-start.3 = (f32[1,16,1024]{2,1,0:T(8,128)S(1)}, f32[1,16,1024]{2,1,0:T(8,128)}, u32[]{:S(2)}) copy-start(f32[1,16,1024]{2,1,0:T(8,128)} %param.13) | copy-start | bytes 196612
  3.9 0.7 %copy-start.5 = (f32[1,1024]{1,0:T(1,128)S(1)}, f32[1,1024]{1,0:T(1,128)}, u32[]{:S(2)}) copy-start(f32[1,1024]{1,0:T(1,128)} %retain_ref.3) | copy-start | bytes 12292
  4.6 0.7 %copy-start.7 = (s32[1,8]{1,0:T(1,128)S(1)}, s32[1,8]{1,0:T(1,128)}, u32[]{:S(2)}) copy-start(s32[1,8]{1,0:T(1,128)} %partner_ref.3) | copy-start | bytes 100
  5.2 0.7 %copy-start.9 = (s32[1,8]{1,0:T(1,128)S(1)}, s32[1,8]{1,0:T(1,128)}, u32[]{:S(2)}) copy-start(s32[1,8]{1,0:T(1,128)} %live_ref.3) | copy-start | bytes 100
  5.9 0.7 %copy-start.11 = (f32[1,8]{1,0:T(1,128)S(1)}, f32[1,8]{1,0:T(1,128)}, u32[]{:S(2)}) copy-start(f32[1,8]{1,0:T(1,128)} %admittance_ref.3) | copy-start | bytes 100
  6.5 0.7 %copy-start.13 = (s32[1,8]{1,0:T(1,128)S(1)}, s32[1,8]{1,0:T(1,128)}, u32[]{:S(2)}) copy-start(s32[1,8]{1,0:T(1,128)} %block_ref.1) | copy-start | bytes 100
  7.2 12.7 %copy-start.2 = (f32[1,1,16,1024]{3,2,1,0:T(8,128)S(1)}, f32[1,1,16,1024]{3,2,1,0:T(8,128)}, u32[]{:S(2)}) copy-start(f32[1,1,16,1024]{3,2,1,0:T(8,128)} %param.10) | copy-start | bytes 196612
  7.2 12.7 %copy-start.4 = (f32[1,16,1024]{2,1,0:T(8,128)S(1)}, f32[1,16,1024]{2,1,0:T(8,128)}, u32[]{:S(2)}) copy-start(f32[1,16,1024]{2,1,0:T(8,128)} %param.13) | copy-start | bytes 196612
  7.2 12.7 %copy-start.6 = (f32[1,1024]{1,0:T(1,128)S(1)}, f32[1,1024]{1,0:T(1,128)}, u32[]{:S(2)}) copy-start(f32[1,1024]{1,0:T(1,128)} %decay_ref.3) | copy-start | bytes 12292
  11.2 6.1 %collective-permute-start.2 = (f32[96,128]{1,0:T(8,128)S(1)}, f32[96,128]{1,0:T(8,128)S(1)}, u32[]{:S(2)}, u32[]{:S(2)}) collective-permute-start(f32[96,128]{1,0:T(8,128)S(1)} %get-tuple-element.12), channel_id=1, source_target_pairs={{0,6},{1,7},{2,4},{3,5},{4,2},{5,3},{6,0},{7,1},{8,14},{9,15},{10,... | collective-permute-start | bytes 147464 | tf_op jit(solution)/shard_map/ppermute | solution.py:221
  15.2 4.1 %collective-permute-start.1 = (f32[96,128]{1,0:T(8,128)S(1)}, f32[96,128]{1,0:T(8,128)S(1)}, u32[]{:S(2)}, u32[]{:S(2)}) collective-permute-start(f32[96,128]{1,0:T(8,128)S(1)} %get-tuple-element.12), channel_id=1, source_target_pairs={{0,4},{1,5},{2,6},{3,7},{4,0},{5,1},{6,2},{7,3},{8,12},{9,13},{10,... | collective-permute-start | bytes 147464 | tf_op jit(solution)/shard_map/ppermute | solution.py:221
  15.7 4.1 %collective-permute-start = (f32[96,128]{1,0:T(8,128)S(1)}, f32[96,128]{1,0:T(8,128)S(1)}, u32[]{:S(2)}, u32[]{:S(2)}) collective-permute-start(f32[96,128]{1,0:T(8,128)S(1)} %get-tuple-element.12), channel_id=1, source_target_pairs={{0,2},{1,3},{2,0},{3,1},{4,6},{5,7},{6,4},{7,5},{8,10},{9,11},{10,... | collective-permute-start | bytes 147464 | tf_op jit(solution)/shard_map/ppermute | solution.py:221
  19.8 4.4 %collective-permute-start.3 = (f32[4,96,128]{2,1,0:T(8,128)S(1)}, f32[4,96,128]{2,1,0:T(8,128)S(1)}, u32[]{:S(2)}, u32[]{:S(2)}) collective-permute-start(f32[4,96,128]{2,1,0:T(8,128)S(1)} %pad_maximum_fusion.here_ref), channel_id=1, source_target_pairs={{0,1},{1,0},{2,3},{3,2},{4,5},{5,4},{6,7},{7,6},{8,9},{9,8},{10,11... | collective-permute-start | bytes 589832 | tf_op jit(solution)/shard_map/ppermute | solution.py:221
  19.9 4.3 %copy-start.8 = (s32[1,8]{1,0:T(1,128)S(1)}, s32[1,8]{1,0:T(1,128)}, u32[]{:S(2)}) copy-start(s32[1,8]{1,0:T(1,128)} %partner_ref.3) | copy-start | bytes 100
  19.9 4.3 %copy-start.10 = (s32[1,8]{1,0:T(1,128)S(1)}, s32[1,8]{1,0:T(1,128)}, u32[]{:S(2)}) copy-start(s32[1,8]{1,0:T(1,128)} %live_ref.3) | copy-start | bytes 100
  19.9 4.3 %copy-start.12 = (f32[1,8]{1,0:T(1,128)S(1)}, f32[1,8]{1,0:T(1,128)}, u32[]{:S(2)}) copy-start(f32[1,8]{1,0:T(1,128)} %admittance_ref.3) | copy-start | bytes 100
  19.9 4.3 %copy-start.14 = (s32[1,8]{1,0:T(1,128)S(1)}, s32[1,8]{1,0:T(1,128)}, u32[]{:S(2)}) copy-start(s32[1,8]{1,0:T(1,128)} %delay_ref.1) | copy-start | bytes 100
  25.7 6.6 %collective-permute-start.6 = (f32[16,1024]{1,0:T(8,128)S(1)}, f32[16,1024]{1,0:T(8,128)S(1)}, u32[]{:S(2)}, u32[]{:S(2)}) collective-permute-start(f32[16,1024]{1,0:T(8,128)S(1)} %last.1.refs_0_), channel_id=1, source_target_pairs={{0,24},{8,16},{16,8},{24,0},{1,25},{9,17},{17,9},{25,1},{2,26},{10... | collective-permute-start | bytes 196616 | tf_op jit(solution)/shard_map/ppermute | solution.py:221
  29.4 6.1 %collective-permute-start.5 = (f32[16,1024]{1,0:T(8,128)S(1)}, f32[16,1024]{1,0:T(8,128)S(1)}, u32[]{:S(2)}, u32[]{:S(2)}) collective-permute-start(f32[16,1024]{1,0:T(8,128)S(1)} %last.1.refs_0_), channel_id=1, source_target_pairs={{0,16},{8,24},{16,0},{24,8},{1,17},{9,25},{17,1},{25,9},{2,18},{10... | collective-permute-start | bytes 196616 | tf_op jit(solution)/shard_map/ppermute | solution.py:221
  29.4 6.1 %collective-permute-start.4 = (f32[16,1024]{1,0:T(8,128)S(1)}, f32[16,1024]{1,0:T(8,128)S(1)}, u32[]{:S(2)}, u32[]{:S(2)}) collective-permute-start(f32[16,1024]{1,0:T(8,128)S(1)} %last.1.refs_0_), channel_id=1, source_target_pairs={{0,8},{8,0},{16,24},{24,16},{1,9},{9,1},{17,25},{25,17},{2,10},{10... | collective-permute-start | bytes 196616 | tf_op jit(solution)/shard_map/ppermute | solution.py:221

commit v2 on v1

v2 whole, which is shorter than its diff:
```python
import functools

import jax
import jax.numpy as jnp
from jax import lax
from jax.experimental import pallas as pl
from jax.experimental.pallas import tpu as pltpu
from jax.sharding import PartitionSpec as P

TERM = 8
CHUNKS = 4

f32 = jnp.float32
bf16 = jnp.bfloat16
ROWS_BY_ROWS = (((1,), (1,)), ((), ()))


def split(value):
    high = value.astype(bf16)
    return high, (value - high.astype(f32)).astype(bf16)


def stacked(value):
    return jnp.concatenate(split(value), axis=0)


def folded(value):
    half = value.shape[0] // 2
    return value[:half] + value[half:]


def times_rows(left, high, low):
    return lax.dot_general(left, high, ROWS_BY_ROWS, preferred_element_type=f32) + lax.dot_general(
        left, low, ROWS_BY_ROWS, preferred_element_type=f32
    )


def times(left, right):
    return jnp.dot(left, right, preferred_element_type=f32)


def slot_lanes(lines, width, read):
    slot = lax.broadcasted_iota(jnp.int32, (1, width), 1) // TERM % lines
    row = jnp.full((1, width), read(0))
    for line in range(1, lines):
        row = jnp.where(slot == line, read(line), row)
    return row


def prepare_kernel(
    block_hbm, partner_hbm, live_hbm, admittance_hbm, source_hbm, retain_hbm, inverse_hbm,
    high_ref, low_ref, probe_high_ref, probe_low_ref, answer_ref, shift_ref,
    block_ref, partner_ref, live_ref, admittance_ref, source_ref, retain_ref, held, picked,
    landed, arrived, fetched,
):
    nodes = inverse_hbm.shape[0]
    lines = block_ref.shape[1]
    points = lines * TERM
    depth = nodes // CHUNKS
    small = [
        pltpu.make_async_copy(source, target, landed.at[place])
        for place, (source, target) in enumerate(
            [
                (block_hbm, block_ref),
                (partner_hbm, partner_ref),
                (live_hbm, live_ref),
                (admittance_hbm, admittance_ref),
                (source_hbm, source_ref),
                (retain_hbm, retain_ref),
            ]
        )
    ]
    for copy in small:
        copy.start()
    copies = []
    for part in range(CHUNKS):
        rows = pl.ds(part * depth, depth)
        copies.append(
            pltpu.make_async_copy(inverse_hbm.at[rows], held.at[rows], arrived.at[part])
        )
        copies[-1].start()
    small[0].wait()
    rows_wanted = []
    for line in range(lines):
        rows_wanted.append(
            pltpu.make_async_copy(
                inverse_hbm.at[pl.ds(pl.multiple_of(block_ref[0, line] * TERM, TERM), TERM)],
                picked.at[pl.ds(line * TERM, TERM)],
                fetched.at[line],
            )
        )
        rows_wanted[-1].start()
    offset = lax.broadcasted_iota(jnp.int32, (TERM, nodes), 1) - lax.broadcasted_iota(
        jnp.int32, (TERM, nodes), 0
    )
    chosen = jnp.concatenate(
        [(offset == block_ref[0, line] * TERM).astype(f32) for line in range(lines)], axis=0
    ).astype(bf16)
    for copy in small[1:] + rows_wanted:
        copy.wait()
    near = picked[...]
    left = stacked(near * retain_ref[...])
    total = jnp.zeros((2 * points, nodes), f32)
    for part in range(CHUNKS):
        copies[part].wait()
        rows = pl.ds(part * depth, depth)
        high, low = split(held[rows, :])
        high_ref[rows, :] = high
        low_ref[rows, :] = low
        piece = left[:, part * depth : (part + 1) * depth]
        total = total + times(piece, high) + times(piece, low)
    beyond = folded(total)
    near_high, near_low = split(near)
    beyond_high, beyond_low = split(beyond)
    probe_high_ref[:points, :] = chosen
    probe_high_ref[points : 2 * points, :] = jnp.zeros_like(chosen)
    probe_high_ref[2 * points : 3 * points, :] = near_high
    probe_high_ref[3 * points :, :] = beyond_high
    probe_low_ref[: 2 * points, :] = jnp.zeros((2 * points, nodes), bf16)
    probe_low_ref[2 * points : 3 * points, :] = near_low
    probe_low_ref[3 * points :, :] = beyond_low
    blank = jnp.zeros_like(chosen)
    shift_ref[...] = folded(
        times_rows(
            stacked(source_ref[...]),
            jnp.concatenate([blank, near_high], axis=0),
            jnp.concatenate([blank, near_low], axis=0),
        )
    )
    answers = times_rows(chosen, *split(jnp.concatenate([near, near + beyond], axis=0)))
    for line in range(lines):
        weight = admittance_ref[0, line] * live_ref[0, line].astype(f32)
        rows = slice(line * TERM, (line + 1) * TERM)
        answer_ref[rows, :] = weight * answers[rows]
    table = slot_lanes(lines, 2 * points, lambda line: partner_ref[0, line] * TERM)
    table = table + lax.broadcasted_iota(jnp.int32, table.shape, 1) % TERM
    answer_ref[points:, :] = jnp.broadcast_to(table.astype(f32), (TERM, 2 * points))


def package_kernel(count, source_ref, retain_ref, probe_high_ref, probe_low_ref, answer_ref, shift_ref, *refs):
    starts, package_ref = refs[:count], refs[count]
    cols, width = shift_ref.shape
    start = jnp.concatenate([ref[...] for ref in starts], axis=0)
    source = jnp.concatenate([source_ref[...]] * count, axis=0)
    driven = retain_ref[...] * start + source
    terms = folded(
        lax.dot_general(
            stacked(start), probe_high_ref[:width, :], ROWS_BY_ROWS, preferred_element_type=f32
        )
    )
    later = folded(
        times_rows(stacked(driven), probe_high_ref[width:, :], probe_low_ref[width:, :])
    )
    rows = count * cols
    package_ref[:rows, :] = terms
    package_ref[rows : 2 * rows, :] = later + jnp.concatenate([shift_ref[...]] * count, axis=0)
    package_ref[2 * rows :, :] = answer_ref[...]


def advance_kernel(count, turns, high_ref, low_ref, probe_ref, source_ref, retain_ref, *refs):
    starts = refs[:count]
    state_ref, replies_ref = refs[count:]
    points = probe_ref.shape[0] // 4
    rows = count * source_ref.shape[0]
    retain = retain_ref[...]
    source = jnp.concatenate([source_ref[...]] * count, axis=0)
    start = jnp.concatenate([ref[...] for ref in starts], axis=0)
    high, low = high_ref[...], low_ref[...]
    left = jnp.concatenate([stacked(retain * start + source), probe_ref[:points, :]], axis=0)
    out = times_rows(left, high, low)
    state = jnp.concatenate([folded(out[: 2 * rows]), out[2 * rows :]], axis=0)
    for turn in range(turns):
        replies_ref[turn * points : (turn + 1) * points, :] = state[rows:]
        driven = jnp.concatenate(
            [retain * state[:rows] + source, retain * state[rows:]], axis=0
        )
        state = folded(times_rows(stacked(driven), high, low))
    state_ref[...] = state


def finish_kernel(
    count, high_ref, low_ref, state_ref, replies_ref, source_ref, retain_ref, decay_ref, *refs
):
    starts = refs[:count]
    base_ref, reply_high_ref, reply_low_ref, partial = refs[count:]
    cols, nodes = source_ref.shape
    rows = count * cols
    points = state_ref.shape[0] - rows
    retain = retain_ref[...]
    decay = decay_ref[...]
    source = jnp.concatenate([source_ref[...]] * count, axis=0)
    state = state_ref[...]
    driven = jnp.concatenate([retain * state[:rows] + source, retain * state[rows:]], axis=0)
    final = folded(times_rows(stacked(driven), high_ref[...], low_ref[...]))
    start = jnp.concatenate([ref[...] for ref in starts], axis=0)
    partial[...] = final[:rows] - decay * start
    mine = lax.axis_index("tm")
    first = pl.ds(pl.multiple_of(mine * cols, cols), cols)
    total = partial[first, :]
    seed = starts[0][...]
    for place in range(1, count):
        seed = jnp.where(mine == place, starts[place][...], seed)
    total = total + decay * seed
    for turn in range(1, count):
        value = partial[pl.ds(pl.multiple_of((mine ^ turn) * cols, cols), cols), :]
        total = jnp.where(turn <= mine, decay * total + value, total)
    base_ref[...] = total
    reply = jnp.concatenate(
        [
            final[rows:] + state[rows:],
            jnp.zeros((points, nodes), f32),
            replies_ref[points : 2 * points, :],
            replies_ref[:points, :],
        ],
        axis=0,
    )
    reply_high_ref[...], reply_low_ref[...] = split(reply)


def last_kernel(
    subs, count, partner_ref, delay_ref, live_ref, admittance_ref, here_ref, there_ref, base_ref,
    decay_ref, reply_high_ref, reply_low_ref, out_ref, partial,
):
    cols, nodes = base_ref.shape
    lines = partner_ref.shape[1]
    points = lines * TERM
    width = 2 * points
    rows = count * cols
    mine = lax.axis_index("sub")
    lane = lax.broadcasted_iota(jnp.int32, (rows, width), 1)
    pairs = []
    tables = []
    for pair in range(subs // 2):
        odd = pltpu.roll(there_ref[pair, :rows, :], points, 1)
        pairs.append(jnp.where(lane < points, here_ref[pair, :rows, :], odd))
        tables.append(
            jnp.where(
                lane[:TERM] < points,
                here_ref[pair, 2 * rows + points :, :],
                there_ref[pair, 2 * rows + points :, :],
            )[:1]
        )
    snapshot = jnp.concatenate(pairs, axis=1)
    table = jnp.concatenate(tables, axis=1).astype(jnp.int32) ^ (mine * points)
    total = subs * points
    route = (lax.broadcasted_iota(jnp.int32, (total, total), 0) == table).astype(f32).astype(bf16)
    far = folded(times(stacked(snapshot), route))
    later = []
    for pair in range(subs // 2):
        both = far[:, pair * width : (pair + 1) * width]
        left = jnp.concatenate(
            [
                stacked(jnp.where(lane < points, both, 0.0)),
                stacked(jnp.where(lane < points, 0.0, both)),
            ],
            axis=0,
        )
        answers = jnp.concatenate(
            [
                here_ref[pair, 2 * rows : 2 * rows + points, :],
                there_ref[pair, 2 * rows : 2 * rows + points, :],
            ],
            axis=0,
        )
        high, low = split(answers)
        sums = times(left, high) + times(left, low)
        later.append(here_ref[pair, rows : 2 * rows, :] + folded(sums[: 2 * rows]))
        later.append(there_ref[pair, rows : 2 * rows, :] + folded(sums[2 * rows :]))
    known = jnp.concatenate(later + [snapshot], axis=1)
    delay = slot_lanes(lines, width, lambda line: delay_ref[0, line])
    slot = slot_lanes(lines, width, lambda line: partner_ref[0, line])
    weight = slot_lanes(
        lines, width, lambda line: admittance_ref[0, line] * live_ref[0, line].astype(f32)
    )
    index = lax.broadcasted_iota(jnp.int32, (1, width), 1)
    source = (slot * TERM + index % TERM) ^ (mine * points)
    late = index >= points
    start = source // points * width + source % points
    wanted = jnp.where(
        late,
        jnp.where(delay == 2, start + points, jnp.where(delay == 3, start, subs * width + source)),
        jnp.where(delay == 2, start, subs * width + source),
    )
    pick = lax.broadcasted_iota(jnp.int32, (known.shape[1], width), 0) == wanted
    chosen = folded(times(stacked(known), pick.astype(f32).astype(bf16)))
    first = jnp.where(lane < points, far[:, :width], 0.0)
    left = stacked(jnp.concatenate([weight * first, weight * chosen], axis=1))
    partial[...] = folded(times(left, reply_high_ref[...]) + times(left, reply_low_ref[...]))
    decay = decay_ref[...]
    place = lax.axis_index("tm")
    total = partial[pl.ds(pl.multiple_of(place * cols, cols), cols), :]
    for turn in range(1, count):
        value = partial[pl.ds(pl.multiple_of((place ^ turn) * cols, cols), cols), :]
        total = jnp.where(turn <= place, decay * total + value, total)
    out_ref[...] = base_ref[...] + total


def exchanged(value, axis, count, flip):
    return lax.ppermute(value, axis, [(source, source ^ flip) for source in range(count)])


VMEM = pl.BlockSpec(memory_space=pltpu.VMEM)
SMEM = pl.BlockSpec(memory_space=pltpu.SMEM)
HBM = pl.BlockSpec(memory_space=pltpu.HBM)


def shards(
    slices, subs, starts, inverses, retain, sources, coarse_decay, admittance, partner,
    line_delay, line_live, term_block,
):
    cols, nodes = starts.shape[2:]
    lines = partner.shape[1]
    points = lines * TERM
    width = 2 * points
    rows = slices * cols
    start = starts.reshape(cols, nodes)
    source = sources.reshape(cols, nodes)
    inverse = inverses.reshape(nodes, nodes)
    shape = jax.ShapeDtypeStruct
    begun = [start] + [exchanged(start, "tm", slices, flip) for flip in range(1, slices)]
    high, low, probe_high, probe_low, answer, shift = pl.pallas_call(
        prepare_kernel,
        out_shape=(
            shape((nodes, nodes), bf16),
            shape((nodes, nodes), bf16),
            shape((4 * points, nodes), bf16),
            shape((4 * points, nodes), bf16),
            shape((points + TERM, width), f32),
            shape((cols, width), f32),
        ),
        in_specs=[HBM] * 7,
        out_specs=(VMEM,) * 6,
        scratch_shapes=[
            pltpu.SMEM((1, lines), jnp.int32),
            pltpu.SMEM((1, lines), jnp.int32),
            pltpu.SMEM((1, lines), jnp.int32),
            pltpu.SMEM((1, lines), f32),
            pltpu.VMEM((cols, nodes), f32),
            pltpu.VMEM((1, nodes), f32),
            pltpu.VMEM((nodes, nodes), f32),
            pltpu.VMEM((points, nodes), f32),
            pltpu.SemaphoreType.DMA((6,)),
            pltpu.SemaphoreType.DMA((CHUNKS,)),
            pltpu.SemaphoreType.DMA((lines,)),
        ],
        compiler_params=pltpu.CompilerParams(vmem_limit_bytes=24 << 20),
        name="prepare",
    )(
        *[
            pltpu.with_memory_space_constraint(value, pltpu.HBM)
            for value in (term_block, partner, line_live, admittance, source, retain, inverse)
        ]
    )

    package = pl.pallas_call(
        functools.partial(package_kernel, slices),
        out_shape=shape((2 * rows + points + TERM, width), f32),
        in_specs=[VMEM] * (6 + slices),
        out_specs=VMEM,
        compiler_params=pltpu.CompilerParams(vmem_limit_bytes=16 << 20),
        name="package",
    )(source, retain, probe_high, probe_low, answer, shift, *begun)

    state, replies = pl.pallas_call(
        functools.partial(advance_kernel, slices, 2),
        out_shape=(shape((rows + points, nodes), f32), shape((2 * points, nodes), f32)),
        in_specs=[VMEM] * (5 + slices),
        out_specs=(VMEM,) * 2,
        compiler_params=pltpu.CompilerParams(vmem_limit_bytes=24 << 20),
        cost_estimate=pl.CostEstimate(
            flops=12 * nodes * nodes * 256, bytes_accessed=8 * nodes * nodes, transcendentals=0
        ),
        name="advance",
    )(high, low, probe_high, source, retain, *begun)

    here = jnp.stack(
        [package] + [exchanged(package, "sub", subs, flip) for flip in range(2, subs, 2)]
    )
    here, state = lax.optimization_barrier((here, state))
    there = exchanged(here, "sub", subs, 1)

    base, reply_high, reply_low = pl.pallas_call(
        functools.partial(finish_kernel, slices),
        out_shape=(
            shape((cols, nodes), f32),
            shape((4 * points, nodes), bf16),
            shape((4 * points, nodes), bf16),
        ),
        in_specs=[VMEM] * (7 + slices),
        out_specs=(VMEM,) * 3,
        scratch_shapes=[pltpu.VMEM((rows, nodes), f32)],
        compiler_params=pltpu.CompilerParams(vmem_limit_bytes=24 << 20),
        cost_estimate=pl.CostEstimate(
            flops=4 * nodes * nodes * 256, bytes_accessed=4 * nodes * nodes, transcendentals=0
        ),
        name="finish",
    )(high, low, state, replies, source, retain, coarse_decay, *begun)

    ends = pl.pallas_call(
        functools.partial(last_kernel, subs, slices),
        out_shape=shape((cols, nodes), f32),
        in_specs=[SMEM] * 4 + [VMEM] * 6,
        out_specs=VMEM,
        scratch_shapes=[pltpu.VMEM((rows, nodes), f32)],
        compiler_params=pltpu.CompilerParams(vmem_limit_bytes=40 << 20),
        name="last",
    )(
        partner, line_delay, line_live, admittance, here, there, base, coarse_decay,
        reply_high, reply_low,
    )
    return ends.reshape(starts.shape)


def solution(mesh):
    return jax.shard_map(
        functools.partial(shards, mesh.shape["tm"], mesh.shape["sub"]),
        mesh=mesh,
        in_specs=(
            P("tm", "sub", None, None),
            P("sub", None, None),
            P("sub", None),
            P("sub", None, None),
            P("sub", None),
            P("sub", None),
            P("sub", None),
            P("sub", None),
            P("sub", None),
            P("sub", None),
        ),
        out_specs=P("tm", "sub", None, None),
        check_vma=False,
    )
```

time: 36.5 us -> 23.5 us (0.64)
  waiting for transfers between devices: 9.26 us -> 1.92 us
  local copies, waits for them, and re-layouts: 7.21 us -> 0.04 us
  Pallas kernels: 10.4 us -> 11.9 us
    ppermute x7, waiting for transfers between devices: 9.26 us -> 1.92 us  [exchanged(): lax.ppermute(value, axis, [(source, source ^ flip) for source in range(co...]
    unnamed x30 -> x16, local copies, waits for them, and re-layouts: 7.21 us -> 0.04 us
    pallas_call x4 -> x5, Pallas kernels: 10.4 us -> 11.9 us  [the longest x1 4.09 us: shards(): pl.pallas_call(prepare_kernel, out_shape=(shape((nodes, nodes), bf16), sh...]
  transfers between devices with their start and end apart: 7 -> 7, of which waited for: 5 -> 4; matrix products, arithmetic and copies ran while one was open for 0% -> 0% of each run, Pallas kernels for 12% -> 40%
where the time goes in v2:
time: 23.5 us; the launch traced here: 23.3 us
  Pallas kernels  11.9 us (51%)
  starting transfers between devices  9.27 us (39%)
  waiting for transfers between devices  1.92 us (8%)
    ppermute x7, starting transfers between devices, exchanged(): lax.ppermute(value, axis, [(source, source ^ flip) for source in range(co...  9.27 us
    pallas_call x1, Pallas kernels, shards(): pl.pallas_call(prepare_kernel, out_shape=(shape((nodes, nodes), bf16), sh...  4.09 us
    pallas_call x1, Pallas kernels, shards(): pl.pallas_call(functools.partial(advance_kernel, slices, 2), out_shape=(s...  3.73 us
    pallas_call x1, Pallas kernels, shards(): pl.pallas_call(functools.partial(last_kernel, subs, slices), out_shape=sh...  2.27 us
    ppermute x7, waiting for transfers between devices, exchanged(): lax.ppermute(value, axis, [(source, source ^ flip) for source in range(co...  1.92 us
    pallas_call x1, Pallas kernels, shards(): pl.pallas_call(functools.partial(finish_kernel, slices), out_shape=(shape...  1.46 us
  transfers between devices with their start and end apart: 7, of which 4 were waited for; matrix products, arithmetic and copies ran while one was open for 0% of the time, Pallas kernels for 40%

profile of v2, /device:TPU:0, one launch (start us, length us, event | category | flops | bytes accessed | tf_op | source)
XLA Modules:
  0.0 23.3 jit_solution(9154998059083425442)
XLA Ops:
  0.0 5.1 %collective-permute-start.2 = (f32[16,1024]{1,0:T(8,128)}, f32[16,1024]{1,0:T(8,128)S(1)}, u32[]{:S(2)}, u32[]{:S(2)}) collective-permute-start(f32[16,1024]{1,0:T(8,128)} %bitcast.13), channel_id=1, source_target_pairs={{0,24},{8,16},{16,8},{24,0},{1,25},{9,17},{17,9},{25,1},{2,26},{10... | collective-permute-start | bytes 196616 | tf_op jit(solution)/shard_map/ppermute | solution.py:299
  5.1 0.0 collective-permute-start.1
  5.1 0.6 %collective-permute-start = (f32[16,1024]{1,0:T(8,128)}, f32[16,1024]{1,0:T(8,128)S(1)}, u32[]{:S(2)}, u32[]{:S(2)}) collective-permute-start(f32[16,1024]{1,0:T(8,128)} %bitcast.15), channel_id=1, source_target_pairs={{0,8},{8,0},{16,24},{24,16},{1,9},{9,1},{17,25},{25,17},{2,10},{10... | collective-permute-start | bytes 196616 | tf_op jit(solution)/shard_map/ppermute | solution.py:299
  5.7 4.1 %prepare.1 = (bf16[1024,1024]{1,0:T(8,128)(2,1)S(1)}, bf16[1024,1024]{1,0:T(8,128)(2,1)S(1)}, bf16[256,1024]{1,0:T(8,128)(2,1)S(1)}, bf16[256,1024]{1,0:T(8,128)...) custom-call(s32[1,8]{1,0:T(1,128)} %block_hbm.1, s32[1,8]{1,0:T(1,128)} %partner_ref.1, s32[1,8]{1,0:T(1,128)} %live_ref.1, ...), custom_call_target="tpu_custom_call" | custom-call | tf_op jit(solution)/shard_map/prepare/pallas_call | solution.py:321
  9.7 0.0 collective-permute-done.2.refs_3_
  9.8 1.1 %collective-permute-done.1.refs_2_ = f32[16,1024]{1,0:T(8,128)S(1)} collective-permute-done((f32[16,1024]{1,0:T(8,128)}, f32[16,1024]{1,0:T(8,128)S(1)}, u32[]{:S(2)}, u32[]{:S(2)}) %collective-permute-start.1) | collective-permute-done | bytes 65568 | tf_op jit(solution)/shard_map/ppermute | solution.py:299
  10.9 0.0 collective-permute-done.refs_1_
  10.9 0.4 %package.1 = f32[200,128]{1,0:T(8,128)S(1)} custom-call(f32[16,1024]{1,0:T(8,128)S(1)} %bitcast.9, f32[1,1024]{1,0:T(1,128)S(1)} %copy-done.2, bf16[256,1024]{1,0:T(8,128)(2,1)S(1)} %get-tuple-element.18.probe_high_ref.probe_ref, bf16[256,1024]{1,0:T(8,128)(2,1)S(1)} %get-tuple-element.19.probe_low_ref, f32[72,128]{1,0:T(8,128)S(1)} %get-tuple-element.20.answer_ref, ...), custom_call_target="tpu_custom_call" | custom-call | tf_op jit(solution)/shard_map/package/pallas_call | solution.py:355
  11.3 2.5 %collective-permute-start.5 = (f32[200,128]{1,0:T(8,128)S(1)}, f32[200,128]{1,0:T(8,128)S(1)}, u32[]{:S(2)}, u32[]{:S(2)}) collective-permute-start(f32[200,128]{1,0:T(8,128)S(1)} %package.1), channel_id=1, source_target_pairs={{0,6},{1,7},{2,4},{3,5},{4,2},{5,3},{6,0},{7,1},{8,14},{9,15},{10,... | collective-permute-start | bytes 307208 | tf_op jit(solution)/shard_map/ppermute | solution.py:299
  13.8 0.5 %collective-permute-start.4 = (f32[200,128]{1,0:T(8,128)S(1)}, f32[200,128]{1,0:T(8,128)S(1)}, u32[]{:S(2)}, u32[]{:S(2)}) collective-permute-start(f32[200,128]{1,0:T(8,128)S(1)} %package.1), channel_id=1, source_target_pairs={{0,4},{1,5},{2,6},{3,7},{4,0},{5,1},{6,2},{7,3},{8,12},{9,13},{10,... | collective-permute-start | bytes 307208 | tf_op jit(solution)/shard_map/ppermute | solution.py:299
  14.3 0.5 %collective-permute-start.3 = (f32[200,128]{1,0:T(8,128)S(1)}, f32[200,128]{1,0:T(8,128)S(1)}, u32[]{:S(2)}, u32[]{:S(2)}) collective-permute-start(f32[200,128]{1,0:T(8,128)S(1)} %package.1), channel_id=1, source_target_pairs={{0,2},{1,3},{2,0},{3,1},{4,6},{5,7},{6,4},{7,5},{8,10},{9,11},{10,... | collective-permute-start | bytes 307208 | tf_op jit(solution)/shard_map/ppermute | solution.py:299
  14.9 3.7 %advance.1 = (f32[128,1024]{1,0:T(8,128)S(1)}, f32[128,1024]{1,0:T(8,128)S(1)}) custom-call(bf16[1024,1024]{1,0:T(8,128)(2,1)S(1)} %get-tuple-element.22.high_ref, bf16[1024,1024]{1,0:T(8,128)(2,1)S(1)} %get-tuple-element.23.low_ref, bf16[256,1024]{1,0:T(8,128)(2,1)S(1)} %get-tuple-element.18.probe_high_ref.probe_ref, f32[16,1024]{1,0:T(8,128)S(1)} %bitcast.10, ...), custom_call_target="tpu_custom_call" | custom-call | flops 3221225472 | bytes 8388608 | tf_op jit(solution)/shard_map/advance/pallas_call | solution.py:364
  18.6 0.0 collective-permute-done.5
  18.6 0.5 %collective-permute-done.4 = f32[200,128]{1,0:T(8,128)S(1)} collective-permute-done((f32[200,128]{1,0:T(8,128)S(1)}, f32[200,128]{1,0:T(8,128)S(1)}, u32[]{:S(2)}, u32[]{:S(2)}) %collective-permute-start.4) | collective-permute-done | bytes 102432 | tf_op jit(solution)/shard_map/ppermute | solution.py:299
  19.1 0.1 collective-permute-done.3
  19.2 0.1 collective-permute-start.6
  19.3 0.0 copy-start.4
  19.3 0.0 copy-start.5
  19.3 0.0 copy-start.6
  19.3 0.0 copy-start.7
  19.4 1.5 %finish.1 = (f32[16,1024]{1,0:T(8,128)S(1)}, bf16[256,1024]{1,0:T(8,128)(2,1)S(1)}, bf16[256,1024]{1,0:T(8,128)(2,1)S(1)}) custom-call(bf16[1024,1024]{1,0:T(8,128)(2,1)S(1)} %get-tuple-element.22.high_ref, bf16[1024,1024]{1,0:T(8,128)(2,1)S(1)} %get-tuple-element.23.low_ref, f32[128,1024]{1,0:T(8,128)S(1)} %get-tuple-element.26.state_ref, ...), custom_call_target="tpu_custom_call" | custom-call | flops 1073741824 | bytes 4194304 | tf_op jit(solution)/shard_map/finish/pallas_call | solution.py:382
  20.8 0.2 collective-permute-done.6.there_ref
  21.0 0.0 copy-done.4
  21.1 2.3 %last.1 = f32[16,1024]{1,0:T(8,128)} custom-call(s32[1,8]{1,0:T(1,128)S(1)} %copy-done.4, s32[1,8]{1,0:T(1,128)S(1)} %copy-done.7, s32[1,8]{1,0:T(1,128)S(1)} %copy-done.5, f32[1,8]{1,0:T(1,128)S(1)} %copy-done.6, f32[4,200,128]{2,1,0:T(8,128)S(1)} %pad_maximum_fusion.here_ref, f32[4,200,128]{2,1,0:T(8,128)S(1)} %collective-permute-done.6.there_ref, ...), custom_call_target="tpu_custom_call" | custom-call | tf_op jit(solution)/shard_map/last/pallas_call | solution.py:399
  (12 shorter events, 0.1 us)
Async XLA Ops:
  0.0 9.8 %collective-permute-start.2 = (f32[16,1024]{1,0:T(8,128)}, f32[16,1024]{1,0:T(8,128)S(1)}, u32[]{:S(2)}, u32[]{:S(2)}) collective-permute-start(f32[16,1024]{1,0:T(8,128)} %bitcast.13), channel_id=1, source_target_pairs={{0,24},{8,16},{16,8},{24,0},{1,25},{9,17},{17,9},{25,1},{2,26},{10... | collective-permute-start | bytes 196616 | tf_op jit(solution)/shard_map/ppermute | solution.py:299
  5.1 5.8 %collective-permute-start.1 = (f32[16,1024]{1,0:T(8,128)}, f32[16,1024]{1,0:T(8,128)S(1)}, u32[]{:S(2)}, u32[]{:S(2)}) collective-permute-start(f32[16,1024]{1,0:T(8,128)} %bitcast.14), channel_id=1, source_target_pairs={{0,16},{8,24},{16,0},{24,8},{1,17},{9,25},{17,1},{25,9},{2,18},{10... | collective-permute-start | bytes 196616 | tf_op jit(solution)/shard_map/ppermute | solution.py:299
  5.1 5.8 %collective-permute-start = (f32[16,1024]{1,0:T(8,128)}, f32[16,1024]{1,0:T(8,128)S(1)}, u32[]{:S(2)}, u32[]{:S(2)}) collective-permute-start(f32[16,1024]{1,0:T(8,128)} %bitcast.15), channel_id=1, source_target_pairs={{0,8},{8,0},{16,24},{24,16},{1,9},{9,1},{17,25},{25,17},{2,10},{10... | collective-permute-start | bytes 196616 | tf_op jit(solution)/shard_map/ppermute | solution.py:299
  5.6 5.2 %copy-start = (f32[1,16,1024]{2,1,0:T(8,128)S(1)}, f32[1,16,1024]{2,1,0:T(8,128)}, u32[]{:S(2)}) copy-start(f32[1,16,1024]{2,1,0:T(8,128)} %param.13) | copy-start | bytes 196612
  5.6 5.2 %copy-start.1 = (f32[1,1,16,1024]{3,2,1,0:T(8,128)S(1)}, f32[1,1,16,1024]{3,2,1,0:T(8,128)}, u32[]{:S(2)}) copy-start(f32[1,1,16,1024]{3,2,1,0:T(8,128)} %param.10) | copy-start | bytes 196612
  5.7 5.3 %copy-start.2 = (f32[1,1024]{1,0:T(1,128)S(1)}, f32[1,1024]{1,0:T(1,128)}, u32[]{:S(2)}) copy-start(f32[1,1024]{1,0:T(1,128)} %retain_ref.5) | copy-start | bytes 12292
  11.3 7.3 %collective-permute-start.5 = (f32[200,128]{1,0:T(8,128)S(1)}, f32[200,128]{1,0:T(8,128)S(1)}, u32[]{:S(2)}, u32[]{:S(2)}) collective-permute-start(f32[200,128]{1,0:T(8,128)S(1)} %package.1), channel_id=1, source_target_pairs={{0,6},{1,7},{2,4},{3,5},{4,2},{5,3},{6,0},{7,1},{8,14},{9,15},{10,... | collective-permute-start | bytes 307208 | tf_op jit(solution)/shard_map/ppermute | solution.py:299
  13.8 5.3 %collective-permute-start.4 = (f32[200,128]{1,0:T(8,128)S(1)}, f32[200,128]{1,0:T(8,128)S(1)}, u32[]{:S(2)}, u32[]{:S(2)}) collective-permute-start(f32[200,128]{1,0:T(8,128)S(1)} %package.1), channel_id=1, source_target_pairs={{0,4},{1,5},{2,6},{3,7},{4,0},{5,1},{6,2},{7,3},{8,12},{9,13},{10,... | collective-permute-start | bytes 307208 | tf_op jit(solution)/shard_map/ppermute | solution.py:299
  14.3 4.9 %collective-permute-start.3 = (f32[200,128]{1,0:T(8,128)S(1)}, f32[200,128]{1,0:T(8,128)S(1)}, u32[]{:S(2)}, u32[]{:S(2)}) collective-permute-start(f32[200,128]{1,0:T(8,128)S(1)} %package.1), channel_id=1, source_target_pairs={{0,2},{1,3},{2,0},{3,1},{4,6},{5,7},{6,4},{7,5},{8,10},{9,11},{10,... | collective-permute-start | bytes 307208 | tf_op jit(solution)/shard_map/ppermute | solution.py:299
  14.9 4.4 %copy-start.3 = (f32[1,1024]{1,0:T(1,128)S(1)}, f32[1,1024]{1,0:T(1,128)}, u32[]{:S(2)}) copy-start(f32[1,1024]{1,0:T(1,128)} %decay_ref.3) | copy-start | bytes 12292
  19.2 1.8 %collective-permute-start.6 = (f32[4,200,128]{2,1,0:T(8,128)S(1)}, f32[4,200,128]{2,1,0:T(8,128)S(1)}, u32[]{:S(2)}, u32[]{:S(2)}) collective-permute-start(f32[4,200,128]{2,1,0:T(8,128)S(1)} %pad_maximum_fusion.here_ref), channel_id=1, source_target_pairs={{0,1},{1,0},{2,3},{3,2},{4,5},{5,4},{6,7},{7,6},{8,9},{9,8},{10,11... | collective-permute-start | bytes 1228808 | tf_op jit(solution)/shard_map/ppermute | solution.py:299
  19.3 1.7 %copy-start.4 = (s32[1,8]{1,0:T(1,128)S(1)}, s32[1,8]{1,0:T(1,128)}, u32[]{:S(2)}) copy-start(s32[1,8]{1,0:T(1,128)} %partner_ref.1) | copy-start | bytes 100
  19.3 1.7 %copy-start.5 = (s32[1,8]{1,0:T(1,128)S(1)}, s32[1,8]{1,0:T(1,128)}, u32[]{:S(2)}) copy-start(s32[1,8]{1,0:T(1,128)} %live_ref.1) | copy-start | bytes 100
  19.3 1.7 %copy-start.6 = (f32[1,8]{1,0:T(1,128)S(1)}, f32[1,8]{1,0:T(1,128)}, u32[]{:S(2)}) copy-start(f32[1,8]{1,0:T(1,128)} %admittance_ref.1) | copy-start | bytes 100
  19.3 1.7 %copy-start.7 = (s32[1,8]{1,0:T(1,128)S(1)}, s32[1,8]{1,0:T(1,128)}, u32[]{:S(2)}) copy-start(s32[1,8]{1,0:T(1,128)} %delay_ref.1) | copy-start | bytes 100

commit v3 on v2

--- a/solution.py
+++ b/solution.py
@@ -48,78 +48,90 @@
 
 
 def prepare_kernel(
-    block_hbm, partner_hbm, live_hbm, admittance_hbm, source_hbm, retain_hbm, inverse_hbm,
-    high_ref, low_ref, probe_high_ref, probe_low_ref, answer_ref, shift_ref,
-    block_ref, partner_ref, live_ref, admittance_ref, source_ref, retain_ref, held, picked,
-    landed, arrived, fetched,
+    subs, block_hbm, partner_hbm, delay_hbm, live_hbm, admittance_hbm, source_hbm, retain_hbm,
+    inverse_hbm, high_ref, low_ref, probe_high_ref, probe_low_ref, answer_ref, shift_ref, plan_ref,
+    block_ref, partner_ref, delay_ref, live_ref, admittance_ref, source_ref, retain_ref, held,
+    picked, landed, arrived, fetched,
 ):
     nodes = inverse_hbm.shape[0]
     lines = block_ref.shape[1]
     points = lines * TERM
+    width = 2 * points
     depth = nodes // CHUNKS
     small = [
         pltpu.make_async_copy(source, target, landed.at[place])
         for place, (source, target) in enumerate(
             [
                 (block_hbm, block_ref),
+                (source_hbm, source_ref),
+                (retain_hbm, retain_ref),
                 (partner_hbm, partner_ref),
+                (delay_hbm, delay_ref),
                 (live_hbm, live_ref),
                 (admittance_hbm, admittance_ref),
-                (source_hbm, source_ref),
-                (retain_hbm, retain_ref),
             ]
         )
     ]
-    for copy in small:
+    pieces = [pl.ds(part * depth, depth) for part in range(CHUNKS)]
+    copies = [
+        pltpu.make_async_copy(inverse_hbm.at[rows], held.at[rows], arrived.at[part])
+        for part, rows in enumerate(pieces)
+    ]
+    for copy in small + copies:
         copy.start()
-    copies = []
-    for part in range(CHUNKS):
-        rows = pl.ds(part * depth, depth)
-        copies.append(
-            pltpu.make_async_copy(inverse_hbm.at[rows], held.at[rows], arrived.at[part])
-        )
-        copies[-1].start()
     small[0].wait()
-    rows_wanted = []
-    for line in range(lines):
-        rows_wanted.append(
-            pltpu.make_async_copy(
-                inverse_hbm.at[pl.ds(pl.multiple_of(block_ref[0, line] * TERM, TERM), TERM)],
-                picked.at[pl.ds(line * TERM, TERM)],
-                fetched.at[line],
-            )
-        )
-        rows_wanted[-1].start()
+    wanted = [
+        pltpu.make_async_copy(
+            inverse_hbm.at[pl.ds(pl.multiple_of(block_ref[0, line] * TERM, TERM), TERM)],
+            picked.at[pl.ds(line * TERM, TERM)],
+            fetched.at[line],
+        )
+        for line in range(lines)
+    ]
+    for copy in wanted:
+        copy.start()
     offset = lax.broadcasted_iota(jnp.int32, (TERM, nodes), 1) - lax.broadcasted_iota(
         jnp.int32, (TERM, nodes), 0
     )
     chosen = jnp.concatenate(
         [(offset == block_ref[0, line] * TERM).astype(f32) for line in range(lines)], axis=0
     ).astype(bf16)
-    for copy in small[1:] + rows_wanted:
+    probe_high_ref[:points, :] = chosen
+    blank = jnp.zeros_like(chosen)
+    for copy in small[1:]:
+        copy.wait()
+    weights = [
+        admittance_ref[0, line] * live_ref[0, line].astype(f32) for line in range(lines)
+    ]
+    index = lax.broadcasted_iota(jnp.int32, (1, width), 1)
+    table = slot_lanes(lines, width, lambda line: partner_ref[0, line] * TERM) + index % TERM
+    answer_ref[points:, :] = jnp.broadcast_to(table.astype(f32), (TERM, width))
+    place = table ^ (lax.axis_index("sub") * points)
+    delay = slot_lanes(lines, width, lambda line: delay_ref[0, line])
+    begin = place // points * width + place % points
+    early = subs * width + place
+    target = jnp.where(
+        index >= points,
+        jnp.where(delay == 2, begin + points, jnp.where(delay == 3, begin, early)),
+        jnp.where(delay == 2, begin, early),
+    )
+    plan_ref[...] = jnp.concatenate(
+        [slot_lanes(lines, width, lambda line: weights[line]), target.astype(f32)], axis=0
+    )
+
+    def keep(part):
+        copies[part].wait()
+        high_ref[pieces[part], :], low_ref[pieces[part], :] = split(held[pieces[part], :])
+
+    for part in range(CHUNKS):
+        keep(part)
+    for copy in wanted:
         copy.wait()
     near = picked[...]
+    near_high, near_low = split(near)
     left = stacked(near * retain_ref[...])
-    total = jnp.zeros((2 * points, nodes), f32)
-    for part in range(CHUNKS):
-        copies[part].wait()
-        rows = pl.ds(part * depth, depth)
-        high, low = split(held[rows, :])
-        high_ref[rows, :] = high
-        low_ref[rows, :] = low
-        piece = left[:, part * depth : (part + 1) * depth]
-        total = total + times(piece, high) + times(piece, low)
-    beyond = folded(total)
-    near_high, near_low = split(near)
-    beyond_high, beyond_low = split(beyond)
-    probe_high_ref[:points, :] = chosen
-    probe_high_ref[points : 2 * points, :] = jnp.zeros_like(chosen)
-    probe_high_ref[2 * points : 3 * points, :] = near_high
-    probe_high_ref[3 * points :, :] = beyond_high
-    probe_low_ref[: 2 * points, :] = jnp.zeros((2 * points, nodes), bf16)
-    probe_low_ref[2 * points : 3 * points, :] = near_low
-    probe_low_ref[3 * points :, :] = beyond_low
-    blank = jnp.zeros_like(chosen)
+    probe_high_ref[points : 2 * points, :] = near_high
+    probe_low_ref[:points, :] = near_low
     shift_ref[...] = folded(
         times_rows(
             stacked(source_ref[...]),
@@ -127,40 +139,50 @@
             jnp.concatenate([blank, near_low], axis=0),
         )
     )
+    total = jnp.zeros((2 * points, nodes), f32)
+    for part in range(CHUNKS):
+        piece = left[:, part * depth : (part + 1) * depth]
+        total = total + times(piece, high_ref[pieces[part], :])
+        total = total + times(piece, low_ref[pieces[part], :])
+    beyond = folded(total)
+    beyond_high, beyond_low = split(beyond)
+    probe_high_ref[2 * points :, :] = beyond_high
+    probe_low_ref[points:, :] = beyond_low
     answers = times_rows(chosen, *split(jnp.concatenate([near, near + beyond], axis=0)))
     for line in range(lines):
-        weight = admittance_ref[0, line] * live_ref[0, line].astype(f32)
         rows = slice(line * TERM, (line + 1) * TERM)
-        answer_ref[rows, :] = weight * answers[rows]
-    table = slot_lanes(lines, 2 * points, lambda line: partner_ref[0, line] * TERM)
-    table = table + lax.broadcasted_iota(jnp.int32, table.shape, 1) % TERM
-    answer_ref[points:, :] = jnp.broadcast_to(table.astype(f32), (TERM, 2 * points))
+        answer_ref[rows, :] = weights[line] * answers[rows]
 
 
 def package_kernel(count, source_ref, retain_ref, probe_high_ref, probe_low_ref, answer_ref, shift_ref, *refs):
     starts, package_ref = refs[:count], refs[count]
     cols, width = shift_ref.shape
+    points = width // 2
     start = jnp.concatenate([ref[...] for ref in starts], axis=0)
     source = jnp.concatenate([source_ref[...]] * count, axis=0)
     driven = retain_ref[...] * start + source
+    chosen = probe_high_ref[:points, :]
     terms = folded(
         lax.dot_general(
-            stacked(start), probe_high_ref[:width, :], ROWS_BY_ROWS, preferred_element_type=f32
-        )
-    )
-    later = folded(
-        times_rows(stacked(driven), probe_high_ref[width:, :], probe_low_ref[width:, :])
-    )
+            stacked(start),
+            jnp.concatenate([chosen, chosen], axis=0),
+            ROWS_BY_ROWS,
+            preferred_element_type=f32,
+        )
+    )
+    later = folded(times_rows(stacked(driven), probe_high_ref[points:, :], probe_low_ref[...]))
     rows = count * cols
-    package_ref[:rows, :] = terms
-    package_ref[rows : 2 * rows, :] = later + jnp.concatenate([shift_ref[...]] * count, axis=0)
-    package_ref[2 * rows :, :] = answer_ref[...]
+    half = rows // 2
+    lane = lax.broadcasted_iota(jnp.int32, (half, width), 1)
+    package_ref[:half, :] = jnp.where(lane < points, terms[:half], terms[half:])
+    package_ref[half : half + rows, :] = later + jnp.concatenate([shift_ref[...]] * count, axis=0)
+    package_ref[half + rows :, :] = answer_ref[...]
 
 
 def advance_kernel(count, turns, high_ref, low_ref, probe_ref, source_ref, retain_ref, *refs):
     starts = refs[:count]
     state_ref, replies_ref = refs[count:]
-    points = probe_ref.shape[0] // 4
+    points = probe_ref.shape[0] // 3
     rows = count * source_ref.shape[0]
     retain = retain_ref[...]
     source = jnp.concatenate([source_ref[...]] * count, axis=0)
@@ -218,33 +240,40 @@
 
 
 def last_kernel(
-    subs, count, partner_ref, delay_ref, live_ref, admittance_ref, here_ref, there_ref, base_ref,
-    decay_ref, reply_high_ref, reply_low_ref, out_ref, partial,
+    subs, count, plan_ref, here_ref, there_ref, base_ref, decay_ref, reply_high_ref, reply_low_ref,
+    out_ref, partial,
 ):
-    cols, nodes = base_ref.shape
-    lines = partner_ref.shape[1]
-    points = lines * TERM
-    width = 2 * points
+    cols, _ = base_ref.shape
+    width = plan_ref.shape[1]
+    points = width // 2
     rows = count * cols
+    half = rows // 2
     mine = lax.axis_index("sub")
     lane = lax.broadcasted_iota(jnp.int32, (rows, width), 1)
     pairs = []
     tables = []
     for pair in range(subs // 2):
-        odd = pltpu.roll(there_ref[pair, :rows, :], points, 1)
-        pairs.append(jnp.where(lane < points, here_ref[pair, :rows, :], odd))
+        even, odd = here_ref[pair, :half, :], there_ref[pair, :half, :]
+        other_even, other_odd = pltpu.roll(even, points, 1), pltpu.roll(odd, points, 1)
+        first = lane[:half] < points
+        pairs.append(
+            jnp.concatenate(
+                [jnp.where(first, even, other_odd), jnp.where(first, other_even, odd)], axis=0
+            )
+        )
         tables.append(
             jnp.where(
                 lane[:TERM] < points,
-                here_ref[pair, 2 * rows + points :, :],
-                there_ref[pair, 2 * rows + points :, :],
+                here_ref[pair, half + rows + points :, :],
+                there_ref[pair, half + rows + points :, :],
             )[:1]
         )
     snapshot = jnp.concatenate(pairs, axis=1)
     table = jnp.concatenate(tables, axis=1).astype(jnp.int32) ^ (mine * points)
     total = subs * points
     route = (lax.broadcasted_iota(jnp.int32, (total, total), 0) == table).astype(f32).astype(bf16)
-    far = folded(times(stacked(snapshot), route))
+    seen = stacked(snapshot)
+    far = folded(times(seen, route))
     later = []
     for pair in range(subs // 2):
         both = far[:, pair * width : (pair + 1) * width]
@@ -257,32 +286,20 @@
         )
         answers = jnp.concatenate(
             [
-                here_ref[pair, 2 * rows : 2 * rows + points, :],
-                there_ref[pair, 2 * rows : 2 * rows + points, :],
+                here_ref[pair, half + rows : half + rows + points, :],
+                there_ref[pair, half + rows : half + rows + points, :],
             ],
             axis=0,
         )
         high, low = split(answers)
         sums = times(left, high) + times(left, low)
-        later.append(here_ref[pair, rows : 2 * rows, :] + folded(sums[: 2 * rows]))
-        later.append(there_ref[pair, rows : 2 * rows, :] + folded(sums[2 * rows :]))
-    known = jnp.concatenate(later + [snapshot], axis=1)
-    delay = slot_lanes(lines, width, lambda line: delay_ref[0, line])
-    slot = slot_lanes(lines, width, lambda line: partner_ref[0, line])
-    weight = slot_lanes(
-        lines, width, lambda line: admittance_ref[0, line] * live_ref[0, line].astype(f32)
-    )
-    index = lax.broadcasted_iota(jnp.int32, (1, width), 1)
-    source = (slot * TERM + index % TERM) ^ (mine * points)
-    late = index >= points
-    start = source // points * width + source % points
-    wanted = jnp.where(
-        late,
-        jnp.where(delay == 2, start + points, jnp.where(delay == 3, start, subs * width + source)),
-        jnp.where(delay == 2, start, subs * width + source),
-    )
-    pick = lax.broadcasted_iota(jnp.int32, (known.shape[1], width), 0) == wanted
-    chosen = folded(times(stacked(known), pick.astype(f32).astype(bf16)))
+        later.append(stacked(here_ref[pair, half : half + rows, :] + folded(sums[: 2 * rows])))
+        later.append(stacked(there_ref[pair, half : half + rows, :] + folded(sums[2 * rows :])))
+    known = jnp.concatenate(later + [seen], axis=1)
+    weight = plan_ref[:1, :]
+    target = plan_ref[1:2, :].astype(jnp.int32)
+    pick = lax.broadcasted_iota(jnp.int32, (known.shape[1], width), 0) == target
+    chosen = folded(times(known, pick.astype(f32).astype(bf16)))
     first = jnp.where(lane < points, far[:, :width], 0.0)
     left = stacked(jnp.concatenate([weight * first, weight * chosen], axis=1))
     partial[...] = folded(times(left, reply_high_ref[...]) + times(left, reply_low_ref[...]))
@@ -300,11 +317,14 @@
 
 
 VMEM = pl.BlockSpec(memory_space=pltpu.VMEM)
-SMEM = pl.BlockSpec(memory_space=pltpu.SMEM)
 HBM = pl.BlockSpec(memory_space=pltpu.HBM)
 
 
-def shards(
+def shards(slices, subs, *arrays):
+    return iterated(slices, subs, *arrays)
+
+
+def iterated(
     slices, subs, starts, inverses, retain, sources, coarse_decay, admittance, partner,
     line_delay, line_live, term_block,
 ):
@@ -317,20 +337,24 @@
     source = sources.reshape(cols, nodes)
     inverse = inverses.reshape(nodes, nodes)
     shape = jax.ShapeDtypeStruct
-    begun = [start] + [exchanged(start, "tm", slices, flip) for flip in range(1, slices)]
-    high, low, probe_high, probe_low, answer, shift = pl.pallas_call(
-        prepare_kernel,
+    begun = [start]
+    for flip in range(1, slices):
+        begun.append(exchanged(start, "tm", slices, flip))
+    high, low, probe_high, probe_low, answer, shift, plan = pl.pallas_call(
+        functools.partial(prepare_kernel, subs),
         out_shape=(
             shape((nodes, nodes), bf16),
             shape((nodes, nodes), bf16),
-            shape((4 * points, nodes), bf16),
-            shape((4 * points, nodes), bf16),
+            shape((3 * points, nodes), bf16),
+            shape((2 * points, nodes), bf16),
             shape((points + TERM, width), f32),
             shape((cols, width), f32),
+            shape((2, width), f32),
         ),
-        in_specs=[HBM] * 7,
-        out_specs=(VMEM,) * 6,
+        in_specs=[HBM] * 8,
+        out_specs=(VMEM,) * 7,
         scratch_shapes=[
+            pltpu.SMEM((1, lines), jnp.int32),
             pltpu.SMEM((1, lines), jnp.int32),
             pltpu.SMEM((1, lines), jnp.int32),
             pltpu.SMEM((1, lines), jnp.int32),
@@ -339,7 +363,7 @@
             pltpu.VMEM((1, nodes), f32),
             pltpu.VMEM((nodes, nodes), f32),
             pltpu.VMEM((points, nodes), f32),
-            pltpu.SemaphoreType.DMA((6,)),
+            pltpu.SemaphoreType.DMA((7,)),
             pltpu.SemaphoreType.DMA((CHUNKS,)),
             pltpu.SemaphoreType.DMA((lines,)),
         ],
@@ -348,13 +372,15 @@
     )(
         *[
             pltpu.with_memory_space_constraint(value, pltpu.HBM)
-            for value in (term_block, partner, line_live, admittance, source, retain, inverse)
+            for value in (
+                term_block, partner, line_delay, line_live, admittance, source, retain, inverse
+            )
         ]
     )
 
     package = pl.pallas_call(
         functools.partial(package_kernel, slices),
-        out_shape=shape((2 * rows + points + TERM, width), f32),
+        out_shape=shape((rows // 2 + rows + points + TERM, width), f32),
         in_specs=[VMEM] * (6 + slices),
         out_specs=VMEM,
         compiler_params=pltpu.CompilerParams(vmem_limit_bytes=16 << 20),
@@ -399,15 +425,12 @@
     ends = pl.pallas_call(
         functools.partial(last_kernel, subs, slices),
         out_shape=shape((cols, nodes), f32),
-        in_specs=[SMEM] * 4 + [VMEM] * 6,
+        in_specs=[VMEM] * 7,
         out_specs=VMEM,
         scratch_shapes=[pltpu.VMEM((rows, nodes), f32)],
         compiler_params=pltpu.CompilerParams(vmem_limit_bytes=40 << 20),
         name="last",
-    )(
-        partner, line_delay, line_live, admittance, here, there, base, coarse_decay,
-        reply_high, reply_low,
-    )
+    )(plan, here, there, base, coarse_decay, reply_high, reply_low)
     return ends.reshape(starts.shape)
 
 

time: 23.5 us -> 22.4 us (0.953)
  Pallas kernels: 11.9 us -> 11.2 us
    pallas_call x5, Pallas kernels: 11.9 us -> 11.2 us  [the longest x1 3.86 us: iterated(): pl.pallas_call(functools.partial(prepare_kernel, subs), out_shape=(shape(...]
  transfers between devices with their start and end apart: 7 -> 7, of which waited for: 4 -> 3; matrix products, arithmetic and copies ran while one was open for 0% -> 0% of each run, Pallas kernels for 40% -> 41%
where the time goes in v3:
time: 22.4 us; the launch traced here: 22.3 us
  Pallas kernels  11.2 us (50%)
  starting transfers between devices  9.27 us (41%)
  waiting for transfers between devices  1.71 us (8%)
    ppermute x7, starting transfers between devices, exchanged(): lax.ppermute(value, axis, [(source, source ^ flip) for source in range(co...  9.27 us
    pallas_call x1, Pallas kernels, iterated(): pl.pallas_call(functools.partial(prepare_kernel, subs), out_shape=(shape(...  3.86 us
    pallas_call x1, Pallas kernels, iterated(): pl.pallas_call(functools.partial(advance_kernel, slices, 2), out_shape=(s...  3.74 us
    ppermute x7, waiting for transfers between devices, exchanged(): lax.ppermute(value, axis, [(source, source ^ flip) for source in range(co...  1.71 us
    pallas_call x1, Pallas kernels, iterated(): pl.pallas_call(functools.partial(last_kernel, subs, slices), out_shape=sh...  1.71 us
    pallas_call x1, Pallas kernels, iterated(): pl.pallas_call(functools.partial(finish_kernel, slices), out_shape=(shape...  1.46 us
  transfers between devices with their start and end apart: 7, of which 3 were waited for; matrix products, arithmetic and copies ran while one was open for 0% of the time, Pallas kernels for 41%

profile of v3, /device:TPU:0, one launch (start us, length us, event | category | flops | bytes accessed | tf_op | source)
XLA Modules:
  0.0 22.3 jit_solution(627870047579951569)
XLA Ops:
  0.0 5.1 %collective-permute-start.2 = (f32[16,1024]{1,0:T(8,128)}, f32[16,1024]{1,0:T(8,128)S(1)}, u32[]{:S(2)}, u32[]{:S(2)}) collective-permute-start(f32[16,1024]{1,0:T(8,128)} %bitcast.13), channel_id=1, source_target_pairs={{0,24},{8,16},{16,8},{24,0},{1,25},{9,17},{17,9},{25,1},{2,26},{10... | collective-permute-start | bytes 196616 | tf_op jit(solution)/shard_map/ppermute | solution.py:316
  5.1 0.0 collective-permute-start.1
  5.1 0.6 %collective-permute-start = (f32[16,1024]{1,0:T(8,128)}, f32[16,1024]{1,0:T(8,128)S(1)}, u32[]{:S(2)}, u32[]{:S(2)}) collective-permute-start(f32[16,1024]{1,0:T(8,128)} %bitcast.15), channel_id=1, source_target_pairs={{0,8},{8,0},{16,24},{24,16},{1,9},{9,1},{17,25},{25,17},{2,10},{10... | collective-permute-start | bytes 196616 | tf_op jit(solution)/shard_map/ppermute | solution.py:316
  5.6 0.0 copy-start
  5.7 3.9 %prepare.1 = (bf16[1024,1024]{1,0:T(8,128)(2,1)S(1)}, bf16[1024,1024]{1,0:T(8,128)(2,1)S(1)}, bf16[192,1024]{1,0:T(8,128)(2,1)S(1)}, bf16[128,1024]{1,0:T(8,128)...) custom-call(s32[1,8]{1,0:T(1,128)} %block_hbm.1, s32[1,8]{1,0:T(1,128)} %partner_hbm.1, ...), custom_call_target="tpu_custom_call" | custom-call | tf_op jit(solution)/shard_map/prepare/pallas_call | solution.py:343
  9.5 0.0 collective-permute-done.2.refs_3_
  9.5 1.4 %collective-permute-done.1.refs_2_ = f32[16,1024]{1,0:T(8,128)S(1)} collective-permute-done((f32[16,1024]{1,0:T(8,128)}, f32[16,1024]{1,0:T(8,128)S(1)}, u32[]{:S(2)}, u32[]{:S(2)}) %collective-permute-start.1) | collective-permute-done | bytes 65568 | tf_op jit(solution)/shard_map/ppermute | solution.py:316
  10.9 0.0 collective-permute-done.refs_1_
  10.9 0.0 copy-done
  10.9 0.0 copy-done.1
  10.9 0.0 copy-done.2
  10.9 0.4 %package.1 = f32[168,128]{1,0:T(8,128)S(1)} custom-call(f32[16,1024]{1,0:T(8,128)S(1)} %bitcast.9, f32[1,1024]{1,0:T(1,128)S(1)} %copy-done.2, bf16[192,1024]{1,0:T(8,128)(2,1)S(1)} %get-tuple-element.20.probe_high_ref.probe_ref, bf16[128,1024]{1,0:T(8,128)(2,1)S(1)} %get-tuple-element.21.probe_low_ref, f32[72,128]{1,0:T(8,128)S(1)} %get-tuple-element.22.answer_ref, ...), custom_call_target="tpu_custom_call" | custom-call | tf_op jit(solution)/shard_map/package/pallas_call | solution.py:381
  11.3 2.5 %collective-permute-start.5 = (f32[168,128]{1,0:T(8,128)S(1)}, f32[168,128]{1,0:T(8,128)S(1)}, u32[]{:S(2)}, u32[]{:S(2)}) collective-permute-start(f32[168,128]{1,0:T(8,128)S(1)} %package.1), channel_id=1, source_target_pairs={{0,6},{1,7},{2,4},{3,5},{4,2},{5,3},{6,0},{7,1},{8,14},{9,15},{10,... | collective-permute-start | bytes 258056 | tf_op jit(solution)/shard_map/ppermute | solution.py:316
  13.8 0.5 %collective-permute-start.4 = (f32[168,128]{1,0:T(8,128)S(1)}, f32[168,128]{1,0:T(8,128)S(1)}, u32[]{:S(2)}, u32[]{:S(2)}) collective-permute-start(f32[168,128]{1,0:T(8,128)S(1)} %package.1), channel_id=1, source_target_pairs={{0,4},{1,5},{2,6},{3,7},{4,0},{5,1},{6,2},{7,3},{8,12},{9,13},{10,... | collective-permute-start | bytes 258056 | tf_op jit(solution)/shard_map/ppermute | solution.py:316
  14.3 0.5 %collective-permute-start.3 = (f32[168,128]{1,0:T(8,128)S(1)}, f32[168,128]{1,0:T(8,128)S(1)}, u32[]{:S(2)}, u32[]{:S(2)}) collective-permute-start(f32[168,128]{1,0:T(8,128)S(1)} %package.1), channel_id=1, source_target_pairs={{0,2},{1,3},{2,0},{3,1},{4,6},{5,7},{6,4},{7,5},{8,10},{9,11},{10,... | collective-permute-start | bytes 258056 | tf_op jit(solution)/shard_map/ppermute | solution.py:316
  14.9 3.7 %advance.1 = (f32[128,1024]{1,0:T(8,128)S(1)}, f32[128,1024]{1,0:T(8,128)S(1)}) custom-call(bf16[1024,1024]{1,0:T(8,128)(2,1)S(1)} %get-tuple-element.24.high_ref, bf16[1024,1024]{1,0:T(8,128)(2,1)S(1)} %get-tuple-element.25.low_ref, bf16[192,1024]{1,0:T(8,128)(2,1)S(1)} %get-tuple-element.20.probe_high_ref.probe_ref, f32[16,1024]{1,0:T(8,128)S(1)} %bitcast.10, ...), custom_call_target="tpu_custom_call" | custom-call | flops 3221225472 | bytes 8388608 | tf_op jit(solution)/shard_map/advance/pallas_call | solution.py:390
  18.6 0.0 collective-permute-done.5
  18.6 0.0 collective-permute-done.4
  18.6 0.2 collective-permute-done.3
  18.8 0.1 collective-permute-start.6
  18.9 0.0 copy-done.3
  18.9 1.5 %finish.1 = (f32[16,1024]{1,0:T(8,128)S(1)}, bf16[256,1024]{1,0:T(8,128)(2,1)S(1)}, bf16[256,1024]{1,0:T(8,128)(2,1)S(1)}) custom-call(bf16[1024,1024]{1,0:T(8,128)(2,1)S(1)} %get-tuple-element.24.high_ref, bf16[1024,1024]{1,0:T(8,128)(2,1)S(1)} %get-tuple-element.25.low_ref, f32[128,1024]{1,0:T(8,128)S(1)} %get-tuple-element.28.state_ref, ...), custom_call_target="tpu_custom_call" | custom-call | flops 1073741824 | bytes 4194304 | tf_op jit(solution)/shard_map/finish/pallas_call | solution.py:408
  20.4 0.2 collective-permute-done.6.there_ref
  20.6 1.7 %last.1 = f32[16,1024]{1,0:T(8,128)} custom-call(f32[2,128]{1,0:T(2,128)S(1)} %get-tuple-element.19.plan_ref, f32[4,168,128]{2,1,0:T(8,128)S(1)} %pad_maximum_fusion.here_ref, f32[4,168,128]{2,1,0:T(8,128)S(1)} %collective-permute-done.6.there_ref, f32[16,1024]{1,0:T(8,128)S(1)} %get-tuple-element.30.base_ref, f32[1,1024]{1,0:T(1,128)S(1)} %copy-done.3, ...), custom_call_target="tpu_custom_call" | custom-call | tf_op jit(solution)/shard_map/last/pallas_call | solution.py:425
  (4 shorter events, 0.0 us)
Async XLA Ops:
  0.0 9.5 %collective-permute-start.2 = (f32[16,1024]{1,0:T(8,128)}, f32[16,1024]{1,0:T(8,128)S(1)}, u32[]{:S(2)}, u32[]{:S(2)}) collective-permute-start(f32[16,1024]{1,0:T(8,128)} %bitcast.13), channel_id=1, source_target_pairs={{0,24},{8,16},{16,8},{24,0},{1,25},{9,17},{17,9},{25,1},{2,26},{10... | collective-permute-start | bytes 196616 | tf_op jit(solution)/shard_map/ppermute | solution.py:316
  5.1 5.8 %collective-permute-start.1 = (f32[16,1024]{1,0:T(8,128)}, f32[16,1024]{1,0:T(8,128)S(1)}, u32[]{:S(2)}, u32[]{:S(2)}) collective-permute-start(f32[16,1024]{1,0:T(8,128)} %bitcast.14), channel_id=1, source_target_pairs={{0,16},{8,24},{16,0},{24,8},{1,17},{9,25},{17,1},{25,9},{2,18},{10... | collective-permute-start | bytes 196616 | tf_op jit(solution)/shard_map/ppermute | solution.py:316
  5.1 5.8 %collective-permute-start = (f32[16,1024]{1,0:T(8,128)}, f32[16,1024]{1,0:T(8,128)S(1)}, u32[]{:S(2)}, u32[]{:S(2)}) collective-permute-start(f32[16,1024]{1,0:T(8,128)} %bitcast.15), channel_id=1, source_target_pairs={{0,8},{8,0},{16,24},{24,16},{1,9},{9,1},{17,25},{25,17},{2,10},{10... | collective-permute-start | bytes 196616 | tf_op jit(solution)/shard_map/ppermute | solution.py:316
  5.6 5.2 %copy-start = (f32[1,16,1024]{2,1,0:T(8,128)S(1)}, f32[1,16,1024]{2,1,0:T(8,128)}, u32[]{:S(2)}) copy-start(f32[1,16,1024]{2,1,0:T(8,128)} %param.13) | copy-start | bytes 196612
  5.6 5.2 %copy-start.1 = (f32[1,1,16,1024]{3,2,1,0:T(8,128)S(1)}, f32[1,1,16,1024]{3,2,1,0:T(8,128)}, u32[]{:S(2)}) copy-start(f32[1,1,16,1024]{3,2,1,0:T(8,128)} %param.10) | copy-start | bytes 196612
  5.7 5.3 %copy-start.2 = (f32[1,1024]{1,0:T(1,128)S(1)}, f32[1,1024]{1,0:T(1,128)}, u32[]{:S(2)}) copy-start(f32[1,1024]{1,0:T(1,128)} %retain_ref.5) | copy-start | bytes 12292
  11.3 7.3 %collective-permute-start.5 = (f32[168,128]{1,0:T(8,128)S(1)}, f32[168,128]{1,0:T(8,128)S(1)}, u32[]{:S(2)}, u32[]{:S(2)}) collective-permute-start(f32[168,128]{1,0:T(8,128)S(1)} %package.1), channel_id=1, source_target_pairs={{0,6},{1,7},{2,4},{3,5},{4,2},{5,3},{6,0},{7,1},{8,14},{9,15},{10,... | collective-permute-start | bytes 258056 | tf_op jit(solution)/shard_map/ppermute | solution.py:316
  13.8 4.8 %collective-permute-start.4 = (f32[168,128]{1,0:T(8,128)S(1)}, f32[168,128]{1,0:T(8,128)S(1)}, u32[]{:S(2)}, u32[]{:S(2)}) collective-permute-start(f32[168,128]{1,0:T(8,128)S(1)} %package.1), channel_id=1, source_target_pairs={{0,4},{1,5},{2,6},{3,7},{4,0},{5,1},{6,2},{7,3},{8,12},{9,13},{10,... | collective-permute-start | bytes 258056 | tf_op jit(solution)/shard_map/ppermute | solution.py:316
  14.3 4.5 %collective-permute-start.3 = (f32[168,128]{1,0:T(8,128)S(1)}, f32[168,128]{1,0:T(8,128)S(1)}, u32[]{:S(2)}, u32[]{:S(2)}) collective-permute-start(f32[168,128]{1,0:T(8,128)S(1)} %package.1), channel_id=1, source_target_pairs={{0,2},{1,3},{2,0},{3,1},{4,6},{5,7},{6,4},{7,5},{8,10},{9,11},{10,... | collective-permute-start | bytes 258056 | tf_op jit(solution)/shard_map/ppermute | solution.py:316
  14.9 4.1 %copy-start.3 = (f32[1,1024]{1,0:T(1,128)S(1)}, f32[1,1024]{1,0:T(1,128)}, u32[]{:S(2)}) copy-start(f32[1,1024]{1,0:T(1,128)} %decay_ref.3) | copy-start | bytes 12292
  18.8 1.7 %collective-permute-start.6 = (f32[4,168,128]{2,1,0:T(8,128)S(1)}, f32[4,168,128]{2,1,0:T(8,128)S(1)}, u32[]{:S(2)}, u32[]{:S(2)}) collective-permute-start(f32[4,168,128]{2,1,0:T(8,128)S(1)} %pad_maximum_fusion.here_ref), channel_id=1, source_target_pairs={{0,1},{1,0},{2,3},{3,2},{4,5},{5,4},{6,7},{7,6},{8,9},{9,8},{10,11... | collective-permute-start | bytes 1032200 | tf_op jit(solution)/shard_map/ppermute | solution.py:316

commit v4 on v3

--- a/solution.py
+++ b/solution.py
@@ -39,6 +39,22 @@
     return jnp.dot(left, right, preferred_element_type=f32)
 
 
+def packs(value, count, lanes):
+    half = value.shape[0] // 2
+    first = lax.broadcasted_iota(jnp.int32, (half, 2 * lanes), 1) < lanes
+    blocks = []
+    for pair in range(count // 2):
+        tile = value[:, pair * 2 * lanes : (pair + 1) * 2 * lanes]
+        turned = pltpu.roll(tile, lanes, 1)
+        blocks.append(jnp.where(first, tile[:half], turned[half:]))
+        blocks.append(jnp.where(first, turned[:half], tile[half:]))
+    return blocks
+
+
+def unpacked(value):
+    return jnp.concatenate([value, pltpu.roll(value, value.shape[1] // 2, 1)], axis=0)
+
+
 def slot_lanes(lines, width, read):
     slot = lax.broadcasted_iota(jnp.int32, (1, width), 1) // TERM % lines
     row = jnp.full((1, width), read(0))
@@ -49,9 +65,9 @@
 
 def prepare_kernel(
     subs, block_hbm, partner_hbm, delay_hbm, live_hbm, admittance_hbm, source_hbm, retain_hbm,
-    inverse_hbm, high_ref, low_ref, probe_high_ref, probe_low_ref, answer_ref, shift_ref, plan_ref,
-    block_ref, partner_ref, delay_ref, live_ref, admittance_ref, source_ref, retain_ref, held,
-    picked, landed, arrived, fetched,
+    inverse_hbm, high_ref, low_ref, chosen_ref, probe_high_ref, probe_low_ref, answer_ref,
+    shift_ref, plan_ref, scale_ref, block_ref, partner_ref, delay_ref, live_ref, admittance_ref, source_ref, retain_ref, held,
+    picked, probe, landed, arrived, fetched,
 ):
     nodes = inverse_hbm.shape[0]
     lines = block_ref.shape[1]
@@ -96,28 +112,48 @@
     chosen = jnp.concatenate(
         [(offset == block_ref[0, line] * TERM).astype(f32) for line in range(lines)], axis=0
     ).astype(bf16)
-    probe_high_ref[:points, :] = chosen
+    chosen_ref[...] = chosen
     blank = jnp.zeros_like(chosen)
+    probe[...] = jnp.zeros_like(probe)
     for copy in small[1:]:
         copy.wait()
     weights = [
         admittance_ref[0, line] * live_ref[0, line].astype(f32) for line in range(lines)
     ]
+    mine = lax.axis_index("sub")
+    room = max(1, 2 * lines // subs)
+    fars = [partner_ref[0, line] for line in range(lines)]
+    owners = [lax.div(far, lines) for far in fars]
+    sent, wanted_rank = [], []
+    for line in range(lines):
+        rank = jnp.int32(0)
+        before = jnp.int32(0)
+        for other in range(lines):
+            if other != line:
+                same = owners[other] == owners[line]
+                smaller = same & (fars[other] < fars[line])
+                rank = rank + jnp.where(smaller, 1, 0)
+            if other < line:
+                before = before + jnp.where(same, 1, 0)
+        block = lax.div(owners[line] ^ mine, 2)
+        run = (owners[line] & 1) * room + jnp.minimum(rank, room - 1)
+        sent.append(block * points + run * TERM)
+        wanted_rank.append(((mine & 1) * room + jnp.minimum(before, room - 1)) * TERM)
     index = lax.broadcasted_iota(jnp.int32, (1, width), 1)
     table = slot_lanes(lines, width, lambda line: partner_ref[0, line] * TERM) + index % TERM
-    answer_ref[points:, :] = jnp.broadcast_to(table.astype(f32), (TERM, width))
-    place = table ^ (lax.axis_index("sub") * points)
+    place = table ^ (mine * points)
     delay = slot_lanes(lines, width, lambda line: delay_ref[0, line])
-    begin = place // points * width + place % points
+    begin = place // points * width + index % TERM
+    begin = begin + slot_lanes(lines, width, lambda line: wanted_rank[line])
     early = subs * width + place
     target = jnp.where(
         index >= points,
-        jnp.where(delay == 2, begin + points, jnp.where(delay == 3, begin, early)),
+        jnp.where(delay == 2, begin + points // 2, jnp.where(delay == 3, begin, early)),
         jnp.where(delay == 2, begin, early),
     )
-    plan_ref[...] = jnp.concatenate(
-        [slot_lanes(lines, width, lambda line: weights[line]), target.astype(f32)], axis=0
-    )
+    plan_ref[...] = target
+    for line in range(lines):
+        scale_ref[line * TERM : (line + 1) * TERM, :] = jnp.full((TERM, width), weights[line])
 
     def keep(part):
         copies[part].wait()
@@ -130,38 +166,63 @@
     near = picked[...]
     near_high, near_low = split(near)
     left = stacked(near * retain_ref[...])
-    probe_high_ref[points : 2 * points, :] = near_high
-    probe_low_ref[:points, :] = near_low
-    shift_ref[...] = folded(
+    for line in range(lines):
+        rows = pl.ds(pl.multiple_of(sent[line], TERM), TERM)
+        probe[rows, :] = near[line * TERM : (line + 1) * TERM]
+    spread = subs // 2 * points
+    lead = lax.broadcasted_iota(jnp.int32, (TERM, spread), 1) - lax.broadcasted_iota(
+        jnp.int32, (TERM, spread), 0
+    )
+    gather = jnp.concatenate(
+        [
+            (lead == sent[line] + kind * (points // 2)).astype(f32)
+            for kind in range(2)
+            for line in range(lines)
+        ],
+        axis=0,
+    ).astype(bf16)
+    fixed = folded(
         times_rows(
             stacked(source_ref[...]),
             jnp.concatenate([blank, near_high], axis=0),
             jnp.concatenate([blank, near_low], axis=0),
         )
     )
+    shift_ref[...] = folded(times(stacked(fixed), gather))
     total = jnp.zeros((2 * points, nodes), f32)
     for part in range(CHUNKS):
         piece = left[:, part * depth : (part + 1) * depth]
         total = total + times(piece, high_ref[pieces[part], :])
         total = total + times(piece, low_ref[pieces[part], :])
     beyond = folded(total)
-    beyond_high, beyond_low = split(beyond)
-    probe_high_ref[2 * points :, :] = beyond_high
-    probe_low_ref[points:, :] = beyond_low
+    for line in range(lines):
+        rows = pl.ds(pl.multiple_of(sent[line] + points // 2, TERM), TERM)
+        probe[rows, :] = beyond[line * TERM : (line + 1) * TERM]
+    probe_high_ref[...], probe_low_ref[...] = split(probe[...])
     answers = times_rows(chosen, *split(jnp.concatenate([near, near + beyond], axis=0)))
-    for line in range(lines):
-        rows = slice(line * TERM, (line + 1) * TERM)
-        answer_ref[rows, :] = weights[line] * answers[rows]
-
-
-def package_kernel(count, source_ref, retain_ref, probe_high_ref, probe_low_ref, answer_ref, shift_ref, *refs):
-    starts, package_ref = refs[:count], refs[count]
-    cols, width = shift_ref.shape
-    points = width // 2
+    answers = jnp.concatenate(
+        [weights[line] * answers[line * TERM : (line + 1) * TERM] for line in range(lines)], axis=0
+    )
+    packed = points // 2
+    told = jnp.broadcast_to(table.astype(f32), (TERM, width))
+    blocks = packs(folded(times(stacked(answers), gather)), subs // 2, points)
+    for place, block in enumerate(blocks):
+        begin = place * (packed + TERM)
+        answer_ref[begin : begin + packed, :] = block
+        answer_ref[begin + packed : begin + packed + TERM, :] = told
+
+
+def package_kernel(
+    count, blocks, source_ref, retain_ref, chosen_ref, probe_high_ref, probe_low_ref, answer_ref,
+    shift_ref, *refs,
+):
+    starts, package_refs = refs[:count], refs[count:]
+    cols = source_ref.shape[0]
+    points = chosen_ref.shape[0]
     start = jnp.concatenate([ref[...] for ref in starts], axis=0)
     source = jnp.concatenate([source_ref[...]] * count, axis=0)
     driven = retain_ref[...] * start + source
-    chosen = probe_high_ref[:points, :]
+    chosen = chosen_ref[...]
     terms = folded(
         lax.dot_general(
             stacked(start),
@@ -170,29 +231,34 @@
             preferred_element_type=f32,
         )
     )
-    later = folded(times_rows(stacked(driven), probe_high_ref[points:, :], probe_low_ref[...]))
-    rows = count * cols
-    half = rows // 2
-    lane = lax.broadcasted_iota(jnp.int32, (half, width), 1)
-    package_ref[:half, :] = jnp.where(lane < points, terms[:half], terms[half:])
-    package_ref[half : half + rows, :] = later + jnp.concatenate([shift_ref[...]] * count, axis=0)
-    package_ref[half + rows :, :] = answer_ref[...]
-
-
-def advance_kernel(count, turns, high_ref, low_ref, probe_ref, source_ref, retain_ref, *refs):
+    later = folded(times_rows(stacked(driven), probe_high_ref[...], probe_low_ref[...]))
+    later = later + jnp.concatenate([shift_ref[...]] * count, axis=0)
+    half = count * cols // 2
+    lane = lax.broadcasted_iota(jnp.int32, (half, 2 * points), 1)
+    terms = jnp.where(lane < points, terms[:half], terms[half:])
+    depth = answer_ref.shape[0] // blocks
+    for place, block in enumerate(packs(later, blocks, points)):
+        package_refs[place][:half, :] = terms
+        package_refs[place][half : 2 * half, :] = block
+        package_refs[place][2 * half :, :] = answer_ref[place * depth : (place + 1) * depth, :]
+
+
+def advance_kernel(count, turns, high_ref, low_ref, chosen_ref, scale_ref, source_ref, retain_ref, *refs):
     starts = refs[:count]
-    state_ref, replies_ref = refs[count:]
-    points = probe_ref.shape[0] // 3
+    state_ref, reply_high_ref, reply_low_ref = refs[count:]
+    points = chosen_ref.shape[0]
     rows = count * source_ref.shape[0]
     retain = retain_ref[...]
     source = jnp.concatenate([source_ref[...]] * count, axis=0)
     start = jnp.concatenate([ref[...] for ref in starts], axis=0)
     high, low = high_ref[...], low_ref[...]
-    left = jnp.concatenate([stacked(retain * start + source), probe_ref[:points, :]], axis=0)
+    left = jnp.concatenate([stacked(retain * start + source), chosen_ref[...]], axis=0)
     out = times_rows(left, high, low)
-    state = jnp.concatenate([folded(out[: 2 * rows]), out[2 * rows :]], axis=0)
+    scale = jnp.concatenate([scale_ref[...]] * (out.shape[1] // scale_ref.shape[1]), axis=1)
+    state = jnp.concatenate([folded(out[: 2 * rows]), scale * out[2 * rows :]], axis=0)
     for turn in range(turns):
-        replies_ref[turn * points : (turn + 1) * points, :] = state[rows:]
+        kept = slice((turns - 1 - turn) * points, (turns - turn) * points)
+        reply_high_ref[kept, :], reply_low_ref[kept, :] = split(state[rows:])
         driven = jnp.concatenate(
             [retain * state[:rows] + source, retain * state[rows:]], axis=0
         )
@@ -201,11 +267,12 @@
 
 
 def finish_kernel(
-    count, high_ref, low_ref, state_ref, replies_ref, source_ref, retain_ref, decay_ref, *refs
+    count, high_ref, low_ref, state_ref, later_high_ref, later_low_ref, source_ref, retain_ref,
+    decay_ref, *refs,
 ):
     starts = refs[:count]
     base_ref, reply_high_ref, reply_low_ref, partial = refs[count:]
-    cols, nodes = source_ref.shape
+    cols, _ = source_ref.shape
     rows = count * cols
     points = state_ref.shape[0] - rows
     retain = retain_ref[...]
@@ -227,16 +294,15 @@
         value = partial[pl.ds(pl.multiple_of((mine ^ turn) * cols, cols), cols), :]
         total = jnp.where(turn <= mine, decay * total + value, total)
     base_ref[...] = total
-    reply = jnp.concatenate(
-        [
-            final[rows:] + state[rows:],
-            jnp.zeros((points, nodes), f32),
-            replies_ref[points : 2 * points, :],
-            replies_ref[:points, :],
-        ],
-        axis=0,
-    )
-    reply_high_ref[...], reply_low_ref[...] = split(reply)
+    high, low = split(final[rows:] + state[rows:])
+    blank = jnp.zeros_like(high)
+    for target, first, later in (
+        (reply_high_ref, high, later_high_ref),
+        (reply_low_ref, low, later_low_ref),
+    ):
+        target[:points, :] = first
+        target[points : 2 * points, :] = blank
+        target[2 * points :, :] = later[...]
 
 
 def last_kernel(
@@ -264,8 +330,8 @@
         tables.append(
             jnp.where(
                 lane[:TERM] < points,
-                here_ref[pair, half + rows + points :, :],
-                there_ref[pair, half + rows + points :, :],
+                here_ref[pair, rows + points // 2 :, :],
+                there_ref[pair, rows + points // 2 :, :],
             )[:1]
         )
     snapshot = jnp.concatenate(pairs, axis=1)
@@ -273,35 +339,30 @@
     total = subs * points
     route = (lax.broadcasted_iota(jnp.int32, (total, total), 0) == table).astype(f32).astype(bf16)
     seen = stacked(snapshot)
-    far = folded(times(seen, route))
+    far = times(seen, route)
+    lane = jnp.concatenate([lane, lane], axis=0)
     later = []
     for pair in range(subs // 2):
         both = far[:, pair * width : (pair + 1) * width]
         left = jnp.concatenate(
+            [jnp.where(lane < points, both, 0.0), jnp.where(lane < points, 0.0, both)], axis=0
+        ).astype(bf16)
+        answers = jnp.concatenate(
             [
-                stacked(jnp.where(lane < points, both, 0.0)),
-                stacked(jnp.where(lane < points, 0.0, both)),
+                unpacked(here_ref[pair, rows : rows + points // 2, :]),
+                unpacked(there_ref[pair, rows : rows + points // 2, :]),
             ],
             axis=0,
         )
-        answers = jnp.concatenate(
-            [
-                here_ref[pair, half + rows : half + rows + points, :],
-                there_ref[pair, half + rows : half + rows + points, :],
-            ],
-            axis=0,
-        )
         high, low = split(answers)
         sums = times(left, high) + times(left, low)
-        later.append(stacked(here_ref[pair, half : half + rows, :] + folded(sums[: 2 * rows])))
-        later.append(stacked(there_ref[pair, half : half + rows, :] + folded(sums[2 * rows :])))
+        later.append(stacked(unpacked(here_ref[pair, half:rows, :]) + folded(sums[: 2 * rows])))
+        later.append(stacked(unpacked(there_ref[pair, half:rows, :]) + folded(sums[2 * rows :])))
     known = jnp.concatenate(later + [seen], axis=1)
-    weight = plan_ref[:1, :]
-    target = plan_ref[1:2, :].astype(jnp.int32)
-    pick = lax.broadcasted_iota(jnp.int32, (known.shape[1], width), 0) == target
-    chosen = folded(times(known, pick.astype(f32).astype(bf16)))
+    pick = lax.broadcasted_iota(jnp.int32, (known.shape[1], width), 0) == plan_ref[...]
+    chosen = times(known, pick.astype(f32).astype(bf16))
     first = jnp.where(lane < points, far[:, :width], 0.0)
-    left = stacked(jnp.concatenate([weight * first, weight * chosen], axis=1))
+    left = jnp.concatenate([first, chosen], axis=1).astype(bf16)
     partial[...] = folded(times(left, reply_high_ref[...]) + times(left, reply_low_ref[...]))
     decay = decay_ref[...]
     place = lax.axis_index("tm")
@@ -340,19 +401,23 @@
     begun = [start]
     for flip in range(1, slices):
         begun.append(exchanged(start, "tm", slices, flip))
-    high, low, probe_high, probe_low, answer, shift, plan = pl.pallas_call(
+    blocks = subs // 2
+    spread = blocks * points
+    high, low, chosen, probe_high, probe_low, answer, shift, plan, scale = pl.pallas_call(
         functools.partial(prepare_kernel, subs),
         out_shape=(
             shape((nodes, nodes), bf16),
             shape((nodes, nodes), bf16),
-            shape((3 * points, nodes), bf16),
-            shape((2 * points, nodes), bf16),
-            shape((points + TERM, width), f32),
-            shape((cols, width), f32),
-            shape((2, width), f32),
+            shape((points, nodes), bf16),
+            shape((spread, nodes), bf16),
+            shape((spread, nodes), bf16),
+            shape((blocks * (points // 2 + TERM), width), f32),
+            shape((cols, spread), f32),
+            shape((1, width), jnp.int32),
+            shape((points, width), f32),
         ),
         in_specs=[HBM] * 8,
-        out_specs=(VMEM,) * 7,
+        out_specs=(VMEM,) * 9,
         scratch_shapes=[
             pltpu.SMEM((1, lines), jnp.int32),
             pltpu.SMEM((1, lines), jnp.int32),
@@ -363,6 +428,7 @@
             pltpu.VMEM((1, nodes), f32),
             pltpu.VMEM((nodes, nodes), f32),
             pltpu.VMEM((points, nodes), f32),
+            pltpu.VMEM((spread, nodes), f32),
             pltpu.SemaphoreType.DMA((7,)),
             pltpu.SemaphoreType.DMA((CHUNKS,)),
             pltpu.SemaphoreType.DMA((lines,)),
@@ -378,30 +444,35 @@
         ]
     )
 
-    package = pl.pallas_call(
-        functools.partial(package_kernel, slices),
-        out_shape=shape((rows // 2 + rows + points + TERM, width), f32),
-        in_specs=[VMEM] * (6 + slices),
-        out_specs=VMEM,
+    packages = pl.pallas_call(
+        functools.partial(package_kernel, slices, blocks),
+        out_shape=(shape((rows + points // 2 + TERM, width), f32),) * blocks,
+        in_specs=[VMEM] * (7 + slices),
+        out_specs=(VMEM,) * blocks,
         compiler_params=pltpu.CompilerParams(vmem_limit_bytes=16 << 20),
         name="package",
-    )(source, retain, probe_high, probe_low, answer, shift, *begun)
-
-    state, replies = pl.pallas_call(
+    )(source, retain, chosen, probe_high, probe_low, answer, shift, *begun)
+
+    state, later_high, later_low = pl.pallas_call(
         functools.partial(advance_kernel, slices, 2),
-        out_shape=(shape((rows + points, nodes), f32), shape((2 * points, nodes), f32)),
-        in_specs=[VMEM] * (5 + slices),
-        out_specs=(VMEM,) * 2,
+        out_shape=(
+            shape((rows + points, nodes), f32),
+            shape((2 * points, nodes), bf16),
+            shape((2 * points, nodes), bf16),
+        ),
+        in_specs=[VMEM] * (6 + slices),
+        out_specs=(VMEM,) * 3,
         compiler_params=pltpu.CompilerParams(vmem_limit_bytes=24 << 20),
         cost_estimate=pl.CostEstimate(
             flops=12 * nodes * nodes * 256, bytes_accessed=8 * nodes * nodes, transcendentals=0
         ),
         name="advance",
-    )(high, low, probe_high, source, retain, *begun)
-
-    here = jnp.stack(
-        [package] + [exchanged(package, "sub", subs, flip) for flip in range(2, subs, 2)]
-    )
+    )(high, low, chosen, scale, source, retain, *begun)
+
+    gathered = [packages[0]]
+    for flip in range(2, subs, 2):
+        gathered.append(exchanged(packages[flip // 2], "sub", subs, flip))
+    here = jnp.stack(gathered)
     here, state = lax.optimization_barrier((here, state))
     there = exchanged(here, "sub", subs, 1)
 
@@ -412,7 +483,7 @@
             shape((4 * points, nodes), bf16),
             shape((4 * points, nodes), bf16),
         ),
-        in_specs=[VMEM] * (7 + slices),
+        in_specs=[VMEM] * (8 + slices),
         out_specs=(VMEM,) * 3,
         scratch_shapes=[pltpu.VMEM((rows, nodes), f32)],
         compiler_params=pltpu.CompilerParams(vmem_limit_bytes=24 << 20),
@@ -420,7 +491,7 @@
             flops=4 * nodes * nodes * 256, bytes_accessed=4 * nodes * nodes, transcendentals=0
         ),
         name="finish",
-    )(high, low, state, replies, source, retain, coarse_decay, *begun)
+    )(high, low, state, later_high, later_low, source, retain, coarse_decay, *begun)
 
     ends = pl.pallas_call(
         functools.partial(last_kernel, subs, slices),

time: 22.4 us -> 23 us (1.027)
  Pallas kernels: 11.2 us -> 12.1 us
  waiting for transfers between devices: 1.71 us -> 1.4 us
    pallas_call x1, Pallas kernels: 3.86 us -> 4.69 us  [iterated(): pl.pallas_call(functools.partial(prepare_kernel, subs), out_shape=(shape(...]
    ppermute x7, waiting for transfers between devices: 1.71 us -> 1.4 us  [exchanged(): lax.ppermute(value, axis, [(source, source ^ flip) for source in range(co...]
    pallas_call x1, Pallas kernels: 0.39 us -> 0.62 us  [iterated(): pl.pallas_call(functools.partial(package_kernel, slices, blocks), out_sha...]
  transfers between devices with their start and end apart: 7 -> 7, of which waited for: 3 -> 3; matrix products, arithmetic and copies ran while one was open for 0% -> 0% of each run, Pallas kernels for 41% -> 43%
where the time goes in v4:
time: 23 us; the launch traced here: 22.9 us
  Pallas kernels  12.1 us (53%)
  starting transfers between devices  9.27 us (40%)
  waiting for transfers between devices  1.4 us (6%)
    ppermute x7, starting transfers between devices, exchanged(): lax.ppermute(value, axis, [(source, source ^ flip) for source in range(co...  9.27 us
    pallas_call x1, Pallas kernels, iterated(): pl.pallas_call(functools.partial(prepare_kernel, subs), out_shape=(shape(...  4.69 us
    pallas_call x1, Pallas kernels, iterated(): pl.pallas_call(functools.partial(advance_kernel, slices, 2), out_shape=(s...  3.75 us
    pallas_call x1, Pallas kernels, iterated(): pl.pallas_call(functools.partial(last_kernel, subs, slices), out_shape=sh...  1.68 us
    ppermute x7, waiting for transfers between devices, exchanged(): lax.ppermute(value, axis, [(source, source ^ flip) for source in range(co...  1.4 us
    pallas_call x1, Pallas kernels, iterated(): pl.pallas_call(functools.partial(finish_kernel, slices), out_shape=(shape...  1.35 us
    pallas_call x1, Pallas kernels, iterated(): pl.pallas_call(functools.partial(package_kernel, slices, blocks), out_sha...  0.62 us
  transfers between devices with their start and end apart: 7, of which 3 were waited for; matrix products, arithmetic and copies ran while one was open for 0% of the time, Pallas kernels for 43%

profile of v4, /device:TPU:0, one launch (start us, length us, event | category | flops | bytes accessed | tf_op | source)
XLA Modules:
  0.0 22.9 jit_solution(12648656529333809983)
XLA Ops:
  0.0 5.1 %collective-permute-start.2 = (f32[16,1024]{1,0:T(8,128)}, f32[16,1024]{1,0:T(8,128)S(1)}, u32[]{:S(2)}, u32[]{:S(2)}) collective-permute-start(f32[16,1024]{1,0:T(8,128)} %bitcast.12), channel_id=1, source_target_pairs={{0,24},{8,16},{16,8},{24,0},{1,25},{9,17},{17,9},{25,1},{2,26},{10... | collective-permute-start | bytes 196616 | tf_op jit(solution)/shard_map/ppermute | solution.py:377
  5.1 0.0 collective-permute-start.1
  5.1 0.6 %collective-permute-start = (f32[16,1024]{1,0:T(8,128)}, f32[16,1024]{1,0:T(8,128)S(1)}, u32[]{:S(2)}, u32[]{:S(2)}) collective-permute-start(f32[16,1024]{1,0:T(8,128)} %bitcast.14), channel_id=1, source_target_pairs={{0,8},{8,0},{16,24},{24,16},{1,9},{9,1},{17,25},{25,17},{2,10},{10... | collective-permute-start | bytes 196616 | tf_op jit(solution)/shard_map/ppermute | solution.py:377
  5.6 0.0 copy-start
  5.7 4.7 %prepare.1 = (bf16[1024,1024]{1,0:T(8,128)(2,1)S(1)}, bf16[1024,1024]{1,0:T(8,128)(2,1)S(1)}, bf16[64,1024]{1,0:T(8,128)(2,1)S(1)}, bf16[256,1024]{1,0:T(8,128)(...) custom-call(s32[1,8]{1,0:T(1,128)} %block_hbm.1, ...), custom_call_target="tpu_custom_call" | custom-call | tf_op jit(solution)/shard_map/prepare/pallas_call | solution.py:406
  10.3 0.0 collective-permute-done.2.refs_3_
  10.4 0.5 %collective-permute-done.1.refs_2_ = f32[16,1024]{1,0:T(8,128)S(1)} collective-permute-done((f32[16,1024]{1,0:T(8,128)}, f32[16,1024]{1,0:T(8,128)S(1)}, u32[]{:S(2)}, u32[]{:S(2)}) %collective-permute-start.1) | collective-permute-done | bytes 65568 | tf_op jit(solution)/shard_map/ppermute | solution.py:377
  10.9 0.0 collective-permute-done.refs_1_
  10.9 0.0 copy-done
  10.9 0.0 copy-done.1
  10.9 0.0 copy-done.2
  10.9 0.6 %package.1 = (f32[104,128]{1,0:T(8,128)S(1)}, f32[104,128]{1,0:T(8,128)S(1)}, f32[104,128]{1,0:T(8,128)S(1)}, f32[104,128]{1,0:T(8,128)S(1)}) custom-call(f32[16,1024]{1,0:T(8,128)S(1)} %bitcast.9, f32[1,1024]{1,0:T(1,128)S(1)} %copy-done.2, bf16[64,1024]{1,0:T(8,128)(2,1)S(1)} %get-tuple-element.27.chosen_ref, ...), custom_call_target="tpu_custom_call" | custom-call | tf_op jit(solution)/shard_map/package/pallas_call | solution.py:447
  11.5 1.6 %collective-permute-start.3 = (f32[104,128]{1,0:T(8,128)S(1)}, f32[104,128]{1,0:T(8,128)S(1)}, u32[]{:S(2)}, u32[]{:S(2)}) collective-permute-start(f32[104,128]{1,0:T(8,128)S(1)} %get-tuple-element.33), channel_id=1, source_target_pairs={{0,2},{1,3},{2,0},{3,1},{4,6},{5,7},{6,4},{7,5},{8,10},{9,11},{10,... | collective-permute-start | bytes 159752 | tf_op jit(solution)/shard_map/ppermute | solution.py:377
  13.1 1.5 %collective-permute-start.4 = (f32[104,128]{1,0:T(8,128)S(1)}, f32[104,128]{1,0:T(8,128)S(1)}, u32[]{:S(2)}, u32[]{:S(2)}) collective-permute-start(f32[104,128]{1,0:T(8,128)S(1)} %get-tuple-element.34), channel_id=1, source_target_pairs={{0,4},{1,5},{2,6},{3,7},{4,0},{5,1},{6,2},{7,3},{8,12},{9,13},{10,... | collective-permute-start | bytes 159752 | tf_op jit(solution)/shard_map/ppermute | solution.py:377
  14.6 0.5 %collective-permute-start.5 = (f32[104,128]{1,0:T(8,128)S(1)}, f32[104,128]{1,0:T(8,128)S(1)}, u32[]{:S(2)}, u32[]{:S(2)}) collective-permute-start(f32[104,128]{1,0:T(8,128)S(1)} %get-tuple-element.35), channel_id=1, source_target_pairs={{0,6},{1,7},{2,4},{3,5},{4,2},{5,3},{6,0},{7,1},{8,14},{9,15},{10,... | collective-permute-start | bytes 159752 | tf_op jit(solution)/shard_map/ppermute | solution.py:377
  15.1 3.7 %advance.1 = (f32[128,1024]{1,0:T(8,128)S(1)}, bf16[128,1024]{1,0:T(8,128)(2,1)S(1)}, bf16[128,1024]{1,0:T(8,128)(2,1)S(1)}) custom-call(bf16[1024,1024]{1,0:T(8,128)(2,1)S(1)} %get-tuple-element.36.high_ref, bf16[1024,1024]{1,0:T(8,128)(2,1)S(1)} %get-tuple-element.37.low_ref, bf16[64,1024]{1,0:T(8,128)(2,1)S(1)} %get-tuple-element.27.chosen_ref, ...), custom_call_target="tpu_custom_call" | custom-call | flops 3221225472 | bytes 8388608 | tf_op jit(solution)/shard_map/advance/pallas_call | solution.py:456
  18.8 0.0 collective-permute-done.3
  18.9 0.0 collective-permute-done.4
  18.9 0.8 %collective-permute-done.5 = f32[104,128]{1,0:T(8,128)S(1)} collective-permute-done((f32[104,128]{1,0:T(8,128)S(1)}, f32[104,128]{1,0:T(8,128)S(1)}, u32[]{:S(2)}, u32[]{:S(2)}) %collective-permute-start.5) | collective-permute-done | bytes 53280 | tf_op jit(solution)/shard_map/ppermute | solution.py:377
  19.7 0.1 collective-permute-start.6
  19.7 0.0 copy-done.3
  19.8 1.3 %finish.1 = (f32[16,1024]{1,0:T(8,128)S(1)}, bf16[256,1024]{1,0:T(8,128)(2,1)S(1)}, bf16[256,1024]{1,0:T(8,128)(2,1)S(1)}) custom-call(bf16[1024,1024]{1,0:T(8,128)(2,1)S(1)} %get-tuple-element.36.high_ref, bf16[1024,1024]{1,0:T(8,128)(2,1)S(1)} %get-tuple-element.37.low_ref, f32[128,1024]{1,0:T(8,128)S(1)} %get-tuple-element.41.state_ref, ...), custom_call_target="tpu_custom_call" | custom-call | flops 1073741824 | bytes 4194304 | tf_op jit(solution)/shard_map/finish/pallas_call | solution.py:479
  21.1 0.1 collective-permute-done.6.there_ref
  21.2 1.7 %last.1 = f32[16,1024]{1,0:T(8,128)} custom-call(s32[1,128]{1,0:T(1,128)S(1)} %get-tuple-element.26.plan_ref, f32[4,104,128]{2,1,0:T(8,128)S(1)} %pad_maximum_fusion.here_ref, f32[4,104,128]{2,1,0:T(8,128)S(1)} %collective-permute-done.6.there_ref, f32[16,1024]{1,0:T(8,128)S(1)} %get-tuple-element.44.base_ref, f32[1,1024]{1,0:T(1,128)S(1)} %copy-done.3, ...), custom_call_target="tpu_custom_call" | custom-call | tf_op jit(solution)/shard_map/last/pallas_call | solution.py:496
  (4 shorter events, 0.0 us)
Async XLA Ops:
  0.0 10.4 %collective-permute-start.2 = (f32[16,1024]{1,0:T(8,128)}, f32[16,1024]{1,0:T(8,128)S(1)}, u32[]{:S(2)}, u32[]{:S(2)}) collective-permute-start(f32[16,1024]{1,0:T(8,128)} %bitcast.12), channel_id=1, source_target_pairs={{0,24},{8,16},{16,8},{24,0},{1,25},{9,17},{17,9},{25,1},{2,26},{10... | collective-permute-start | bytes 196616 | tf_op jit(solution)/shard_map/ppermute | solution.py:377
  5.1 5.8 %collective-permute-start.1 = (f32[16,1024]{1,0:T(8,128)}, f32[16,1024]{1,0:T(8,128)S(1)}, u32[]{:S(2)}, u32[]{:S(2)}) collective-permute-start(f32[16,1024]{1,0:T(8,128)} %bitcast.13), channel_id=1, source_target_pairs={{0,16},{8,24},{16,0},{24,8},{1,17},{9,25},{17,1},{25,9},{2,18},{10... | collective-permute-start | bytes 196616 | tf_op jit(solution)/shard_map/ppermute | solution.py:377
  5.1 5.8 %collective-permute-start = (f32[16,1024]{1,0:T(8,128)}, f32[16,1024]{1,0:T(8,128)S(1)}, u32[]{:S(2)}, u32[]{:S(2)}) collective-permute-start(f32[16,1024]{1,0:T(8,128)} %bitcast.14), channel_id=1, source_target_pairs={{0,8},{8,0},{16,24},{24,16},{1,9},{9,1},{17,25},{25,17},{2,10},{10... | collective-permute-start | bytes 196616 | tf_op jit(solution)/shard_map/ppermute | solution.py:377
  5.6 5.2 %copy-start = (f32[1,16,1024]{2,1,0:T(8,128)S(1)}, f32[1,16,1024]{2,1,0:T(8,128)}, u32[]{:S(2)}) copy-start(f32[1,16,1024]{2,1,0:T(8,128)} %param.13) | copy-start | bytes 196612
  5.6 5.2 %copy-start.1 = (f32[1,1,16,1024]{3,2,1,0:T(8,128)S(1)}, f32[1,1,16,1024]{3,2,1,0:T(8,128)}, u32[]{:S(2)}) copy-start(f32[1,1,16,1024]{3,2,1,0:T(8,128)} %param.10) | copy-start | bytes 196612
  5.7 5.3 %copy-start.2 = (f32[1,1024]{1,0:T(1,128)S(1)}, f32[1,1024]{1,0:T(1,128)}, u32[]{:S(2)}) copy-start(f32[1,1024]{1,0:T(1,128)} %retain_ref.5) | copy-start | bytes 12292
  11.5 7.3 %collective-permute-start.3 = (f32[104,128]{1,0:T(8,128)S(1)}, f32[104,128]{1,0:T(8,128)S(1)}, u32[]{:S(2)}, u32[]{:S(2)}) collective-permute-start(f32[104,128]{1,0:T(8,128)S(1)} %get-tuple-element.33), channel_id=1, source_target_pairs={{0,2},{1,3},{2,0},{3,1},{4,6},{5,7},{6,4},{7,5},{8,10},{9,11},{10,... | collective-permute-start | bytes 159752 | tf_op jit(solution)/shard_map/ppermute | solution.py:377
  13.1 5.8 %collective-permute-start.4 = (f32[104,128]{1,0:T(8,128)S(1)}, f32[104,128]{1,0:T(8,128)S(1)}, u32[]{:S(2)}, u32[]{:S(2)}) collective-permute-start(f32[104,128]{1,0:T(8,128)S(1)} %get-tuple-element.34), channel_id=1, source_target_pairs={{0,4},{1,5},{2,6},{3,7},{4,0},{5,1},{6,2},{7,3},{8,12},{9,13},{10,... | collective-permute-start | bytes 159752 | tf_op jit(solution)/shard_map/ppermute | solution.py:377
  14.6 5.0 %collective-permute-start.5 = (f32[104,128]{1,0:T(8,128)S(1)}, f32[104,128]{1,0:T(8,128)S(1)}, u32[]{:S(2)}, u32[]{:S(2)}) collective-permute-start(f32[104,128]{1,0:T(8,128)S(1)} %get-tuple-element.35), channel_id=1, source_target_pairs={{0,6},{1,7},{2,4},{3,5},{4,2},{5,3},{6,0},{7,1},{8,14},{9,15},{10,... | collective-permute-start | bytes 159752 | tf_op jit(solution)/shard_map/ppermute | solution.py:377
  15.1 4.7 %copy-start.3 = (f32[1,1024]{1,0:T(1,128)S(1)}, f32[1,1024]{1,0:T(1,128)}, u32[]{:S(2)}) copy-start(f32[1,1024]{1,0:T(1,128)} %decay_ref.3) | copy-start | bytes 12292
  19.7 1.5 %collective-permute-start.6 = (f32[4,104,128]{2,1,0:T(8,128)S(1)}, f32[4,104,128]{2,1,0:T(8,128)S(1)}, u32[]{:S(2)}, u32[]{:S(2)}) collective-permute-start(f32[4,104,128]{2,1,0:T(8,128)S(1)} %pad_maximum_fusion.here_ref), channel_id=1, source_target_pairs={{0,1},{1,0},{2,3},{3,2},{4,5},{5,4},{6,7},{7,6},{8,9},{9,8},{10,11... | collective-permute-start | bytes 638984 | tf_op jit(solution)/shard_map/ppermute | solution.py:377

commit v5 on v4

--- a/solution.py
+++ b/solution.py
@@ -143,9 +143,9 @@
     table = slot_lanes(lines, width, lambda line: partner_ref[0, line] * TERM) + index % TERM
     place = table ^ (mine * points)
     delay = slot_lanes(lines, width, lambda line: delay_ref[0, line])
-    begin = place // points * width + index % TERM
+    begin = subs * points + place // points * width + index % TERM
     begin = begin + slot_lanes(lines, width, lambda line: wanted_rank[line])
-    early = subs * width + place
+    early = place
     target = jnp.where(
         index >= points,
         jnp.where(delay == 2, begin + points // 2, jnp.where(delay == 3, begin, early)),
@@ -223,24 +223,21 @@
     source = jnp.concatenate([source_ref[...]] * count, axis=0)
     driven = retain_ref[...] * start + source
     chosen = chosen_ref[...]
-    terms = folded(
-        lax.dot_general(
-            stacked(start),
-            jnp.concatenate([chosen, chosen], axis=0),
-            ROWS_BY_ROWS,
-            preferred_element_type=f32,
-        )
-    )
     later = folded(times_rows(stacked(driven), probe_high_ref[...], probe_low_ref[...]))
     later = later + jnp.concatenate([shift_ref[...]] * count, axis=0)
     half = count * cols // 2
-    lane = lax.broadcasted_iota(jnp.int32, (half, 2 * points), 1)
-    terms = jnp.where(lane < points, terms[:half], terms[half:])
     depth = answer_ref.shape[0] // blocks
     for place, block in enumerate(packs(later, blocks, points)):
-        package_refs[place][:half, :] = terms
         package_refs[place][half : 2 * half, :] = block
         package_refs[place][2 * half :, :] = answer_ref[place * depth : (place + 1) * depth, :]
+    terms = folded(
+        lax.dot_general(
+            stacked(start), chosen, ROWS_BY_ROWS, preferred_element_type=f32
+        )
+    )
+    terms = jnp.concatenate([terms[:half], terms[half:]], axis=1)
+    for ref in package_refs:
+        ref[:half, :] = terms
 
 
 def advance_kernel(count, turns, high_ref, low_ref, chosen_ref, scale_ref, source_ref, retain_ref, *refs):
@@ -358,7 +355,7 @@
         sums = times(left, high) + times(left, low)
         later.append(stacked(unpacked(here_ref[pair, half:rows, :]) + folded(sums[: 2 * rows])))
         later.append(stacked(unpacked(there_ref[pair, half:rows, :]) + folded(sums[2 * rows :])))
-    known = jnp.concatenate(later + [seen], axis=1)
+    known = jnp.concatenate([seen] + later, axis=1)
     pick = lax.broadcasted_iota(jnp.int32, (known.shape[1], width), 0) == plan_ref[...]
     chosen = times(known, pick.astype(f32).astype(bf16))
     first = jnp.where(lane < points, far[:, :width], 0.0)

time: 23 us -> 23 us (level)
  no operation moved by 1% of the time
where the time goes in v5:
time: 23 us; the launch traced here: 22.8 us
  Pallas kernels  12 us (52%)
  starting transfers between devices  9.27 us (40%)
  waiting for transfers between devices  1.41 us (6%)
    ppermute x7, starting transfers between devices, exchanged(): lax.ppermute(value, axis, [(source, source ^ flip) for source in range(co...  9.27 us
    pallas_call x1, Pallas kernels, iterated(): pl.pallas_call(functools.partial(prepare_kernel, subs), out_shape=(shape(...  4.69 us
    pallas_call x1, Pallas kernels, iterated(): pl.pallas_call(functools.partial(advance_kernel, slices, 2), out_shape=(s...  3.74 us
    pallas_call x1, Pallas kernels, iterated(): pl.pallas_call(functools.partial(last_kernel, subs, slices), out_shape=sh...  1.63 us
    ppermute x7, waiting for transfers between devices, exchanged(): lax.ppermute(value, axis, [(source, source ^ flip) for source in range(co...  1.41 us
    pallas_call x1, Pallas kernels, iterated(): pl.pallas_call(functools.partial(finish_kernel, slices), out_shape=(shape...  1.35 us
    pallas_call x1, Pallas kernels, iterated(): pl.pallas_call(functools.partial(package_kernel, slices, blocks), out_sha...  0.63 us
  transfers between devices with their start and end apart: 7, of which 3 were waited for; matrix products, arithmetic and copies ran while one was open for 0% of the time, Pallas kernels for 43%

profile of v5, /device:TPU:0, one launch (start us, length us, event | category | flops | bytes accessed | tf_op | source)
XLA Modules:
  0.0 22.8 jit_solution(18425630556238547370)
XLA Ops:
  0.0 5.1 %collective-permute-start.2 = (f32[16,1024]{1,0:T(8,128)}, f32[16,1024]{1,0:T(8,128)S(1)}, u32[]{:S(2)}, u32[]{:S(2)}) collective-permute-start(f32[16,1024]{1,0:T(8,128)} %bitcast.12), channel_id=1, source_target_pairs={{0,24},{8,16},{16,8},{24,0},{1,25},{9,17},{17,9},{25,1},{2,26},{10... | collective-permute-start | bytes 196616 | tf_op jit(solution)/shard_map/ppermute | solution.py:374
  5.1 0.0 collective-permute-start.1
  5.1 0.6 %collective-permute-start = (f32[16,1024]{1,0:T(8,128)}, f32[16,1024]{1,0:T(8,128)S(1)}, u32[]{:S(2)}, u32[]{:S(2)}) collective-permute-start(f32[16,1024]{1,0:T(8,128)} %bitcast.14), channel_id=1, source_target_pairs={{0,8},{8,0},{16,24},{24,16},{1,9},{9,1},{17,25},{25,17},{2,10},{10... | collective-permute-start | bytes 196616 | tf_op jit(solution)/shard_map/ppermute | solution.py:374
  5.6 0.0 copy-start
  5.7 4.7 %prepare.1 = (bf16[1024,1024]{1,0:T(8,128)(2,1)S(1)}, bf16[1024,1024]{1,0:T(8,128)(2,1)S(1)}, bf16[64,1024]{1,0:T(8,128)(2,1)S(1)}, bf16[256,1024]{1,0:T(8,128)(...) custom-call(s32[1,8]{1,0:T(1,128)} %block_hbm.1, ...), custom_call_target="tpu_custom_call" | custom-call | tf_op jit(solution)/shard_map/prepare/pallas_call | solution.py:403
  10.3 0.0 collective-permute-done.2.refs_3_
  10.4 0.5 %collective-permute-done.1.refs_2_ = f32[16,1024]{1,0:T(8,128)S(1)} collective-permute-done((f32[16,1024]{1,0:T(8,128)}, f32[16,1024]{1,0:T(8,128)S(1)}, u32[]{:S(2)}, u32[]{:S(2)}) %collective-permute-start.1) | collective-permute-done | bytes 65568 | tf_op jit(solution)/shard_map/ppermute | solution.py:374
  10.9 0.0 collective-permute-done.refs_1_
  10.9 0.0 copy-done
  10.9 0.0 copy-done.1
  10.9 0.0 copy-done.2
  10.9 0.6 %package.1 = (f32[104,128]{1,0:T(8,128)S(1)}, f32[104,128]{1,0:T(8,128)S(1)}, f32[104,128]{1,0:T(8,128)S(1)}, f32[104,128]{1,0:T(8,128)S(1)}) custom-call(f32[16,1024]{1,0:T(8,128)S(1)} %bitcast.9, f32[1,1024]{1,0:T(1,128)S(1)} %copy-done.2, bf16[64,1024]{1,0:T(8,128)(2,1)S(1)} %get-tuple-element.27.chosen_ref, ...), custom_call_target="tpu_custom_call" | custom-call | tf_op jit(solution)/shard_map/package/pallas_call | solution.py:444
  11.5 1.6 %collective-permute-start.3 = (f32[104,128]{1,0:T(8,128)S(1)}, f32[104,128]{1,0:T(8,128)S(1)}, u32[]{:S(2)}, u32[]{:S(2)}) collective-permute-start(f32[104,128]{1,0:T(8,128)S(1)} %get-tuple-element.33), channel_id=1, source_target_pairs={{0,2},{1,3},{2,0},{3,1},{4,6},{5,7},{6,4},{7,5},{8,10},{9,11},{10,... | collective-permute-start | bytes 159752 | tf_op jit(solution)/shard_map/ppermute | solution.py:374
  13.1 1.5 %collective-permute-start.4 = (f32[104,128]{1,0:T(8,128)S(1)}, f32[104,128]{1,0:T(8,128)S(1)}, u32[]{:S(2)}, u32[]{:S(2)}) collective-permute-start(f32[104,128]{1,0:T(8,128)S(1)} %get-tuple-element.34), channel_id=1, source_target_pairs={{0,4},{1,5},{2,6},{3,7},{4,0},{5,1},{6,2},{7,3},{8,12},{9,13},{10,... | collective-permute-start | bytes 159752 | tf_op jit(solution)/shard_map/ppermute | solution.py:374
  14.6 0.5 %collective-permute-start.5 = (f32[104,128]{1,0:T(8,128)S(1)}, f32[104,128]{1,0:T(8,128)S(1)}, u32[]{:S(2)}, u32[]{:S(2)}) collective-permute-start(f32[104,128]{1,0:T(8,128)S(1)} %get-tuple-element.35), channel_id=1, source_target_pairs={{0,6},{1,7},{2,4},{3,5},{4,2},{5,3},{6,0},{7,1},{8,14},{9,15},{10,... | collective-permute-start | bytes 159752 | tf_op jit(solution)/shard_map/ppermute | solution.py:374
  15.1 3.7 %advance.1 = (f32[128,1024]{1,0:T(8,128)S(1)}, bf16[128,1024]{1,0:T(8,128)(2,1)S(1)}, bf16[128,1024]{1,0:T(8,128)(2,1)S(1)}) custom-call(bf16[1024,1024]{1,0:T(8,128)(2,1)S(1)} %get-tuple-element.36.high_ref, bf16[1024,1024]{1,0:T(8,128)(2,1)S(1)} %get-tuple-element.37.low_ref, bf16[64,1024]{1,0:T(8,128)(2,1)S(1)} %get-tuple-element.27.chosen_ref, ...), custom_call_target="tpu_custom_call" | custom-call | flops 3221225472 | bytes 8388608 | tf_op jit(solution)/shard_map/advance/pallas_call | solution.py:453
  18.9 0.0 collective-permute-done.3
  18.9 0.0 collective-permute-done.4
  18.9 0.8 %collective-permute-done.5 = f32[104,128]{1,0:T(8,128)S(1)} collective-permute-done((f32[104,128]{1,0:T(8,128)S(1)}, f32[104,128]{1,0:T(8,128)S(1)}, u32[]{:S(2)}, u32[]{:S(2)}) %collective-permute-start.5) | collective-permute-done | bytes 53280 | tf_op jit(solution)/shard_map/ppermute | solution.py:374
  19.7 0.1 collective-permute-start.6
  19.8 0.0 copy-done.3
  19.8 1.4 %finish.1 = (f32[16,1024]{1,0:T(8,128)S(1)}, bf16[256,1024]{1,0:T(8,128)(2,1)S(1)}, bf16[256,1024]{1,0:T(8,128)(2,1)S(1)}) custom-call(bf16[1024,1024]{1,0:T(8,128)(2,1)S(1)} %get-tuple-element.36.high_ref, bf16[1024,1024]{1,0:T(8,128)(2,1)S(1)} %get-tuple-element.37.low_ref, f32[128,1024]{1,0:T(8,128)S(1)} %get-tuple-element.41.state_ref, ...), custom_call_target="tpu_custom_call" | custom-call | flops 1073741824 | bytes 4194304 | tf_op jit(solution)/shard_map/finish/pallas_call | solution.py:476
  21.1 0.1 collective-permute-done.6.there_ref
  21.2 1.6 %last.1 = f32[16,1024]{1,0:T(8,128)} custom-call(s32[1,128]{1,0:T(1,128)S(1)} %get-tuple-element.26.plan_ref, f32[4,104,128]{2,1,0:T(8,128)S(1)} %pad_maximum_fusion.here_ref, f32[4,104,128]{2,1,0:T(8,128)S(1)} %collective-permute-done.6.there_ref, f32[16,1024]{1,0:T(8,128)S(1)} %get-tuple-element.44.base_ref, f32[1,1024]{1,0:T(1,128)S(1)} %copy-done.3, ...), custom_call_target="tpu_custom_call" | custom-call | tf_op jit(solution)/shard_map/last/pallas_call | solution.py:493
  (4 shorter events, 0.0 us)
Async XLA Ops:
  0.0 10.4 %collective-permute-start.2 = (f32[16,1024]{1,0:T(8,128)}, f32[16,1024]{1,0:T(8,128)S(1)}, u32[]{:S(2)}, u32[]{:S(2)}) collective-permute-start(f32[16,1024]{1,0:T(8,128)} %bitcast.12), channel_id=1, source_target_pairs={{0,24},{8,16},{16,8},{24,0},{1,25},{9,17},{17,9},{25,1},{2,26},{10... | collective-permute-start | bytes 196616 | tf_op jit(solution)/shard_map/ppermute | solution.py:374
  5.1 5.8 %collective-permute-start.1 = (f32[16,1024]{1,0:T(8,128)}, f32[16,1024]{1,0:T(8,128)S(1)}, u32[]{:S(2)}, u32[]{:S(2)}) collective-permute-start(f32[16,1024]{1,0:T(8,128)} %bitcast.13), channel_id=1, source_target_pairs={{0,16},{8,24},{16,0},{24,8},{1,17},{9,25},{17,1},{25,9},{2,18},{10... | collective-permute-start | bytes 196616 | tf_op jit(solution)/shard_map/ppermute | solution.py:374
  5.1 5.8 %collective-permute-start = (f32[16,1024]{1,0:T(8,128)}, f32[16,1024]{1,0:T(8,128)S(1)}, u32[]{:S(2)}, u32[]{:S(2)}) collective-permute-start(f32[16,1024]{1,0:T(8,128)} %bitcast.14), channel_id=1, source_target_pairs={{0,8},{8,0},{16,24},{24,16},{1,9},{9,1},{17,25},{25,17},{2,10},{10... | collective-permute-start | bytes 196616 | tf_op jit(solution)/shard_map/ppermute | solution.py:374
  5.6 5.2 %copy-start = (f32[1,16,1024]{2,1,0:T(8,128)S(1)}, f32[1,16,1024]{2,1,0:T(8,128)}, u32[]{:S(2)}) copy-start(f32[1,16,1024]{2,1,0:T(8,128)} %param.13) | copy-start | bytes 196612
  5.6 5.2 %copy-start.1 = (f32[1,1,16,1024]{3,2,1,0:T(8,128)S(1)}, f32[1,1,16,1024]{3,2,1,0:T(8,128)}, u32[]{:S(2)}) copy-start(f32[1,1,16,1024]{3,2,1,0:T(8,128)} %param.10) | copy-start | bytes 196612
  5.7 5.3 %copy-start.2 = (f32[1,1024]{1,0:T(1,128)S(1)}, f32[1,1024]{1,0:T(1,128)}, u32[]{:S(2)}) copy-start(f32[1,1024]{1,0:T(1,128)} %retain_ref.5) | copy-start | bytes 12292
  11.5 7.3 %collective-permute-start.3 = (f32[104,128]{1,0:T(8,128)S(1)}, f32[104,128]{1,0:T(8,128)S(1)}, u32[]{:S(2)}, u32[]{:S(2)}) collective-permute-start(f32[104,128]{1,0:T(8,128)S(1)} %get-tuple-element.33), channel_id=1, source_target_pairs={{0,2},{1,3},{2,0},{3,1},{4,6},{5,7},{6,4},{7,5},{8,10},{9,11},{10,... | collective-permute-start | bytes 159752 | tf_op jit(solution)/shard_map/ppermute | solution.py:374
  13.1 5.8 %collective-permute-start.4 = (f32[104,128]{1,0:T(8,128)S(1)}, f32[104,128]{1,0:T(8,128)S(1)}, u32[]{:S(2)}, u32[]{:S(2)}) collective-permute-start(f32[104,128]{1,0:T(8,128)S(1)} %get-tuple-element.34), channel_id=1, source_target_pairs={{0,4},{1,5},{2,6},{3,7},{4,0},{5,1},{6,2},{7,3},{8,12},{9,13},{10,... | collective-permute-start | bytes 159752 | tf_op jit(solution)/shard_map/ppermute | solution.py:374
  14.6 5.0 %collective-permute-start.5 = (f32[104,128]{1,0:T(8,128)S(1)}, f32[104,128]{1,0:T(8,128)S(1)}, u32[]{:S(2)}, u32[]{:S(2)}) collective-permute-start(f32[104,128]{1,0:T(8,128)S(1)} %get-tuple-element.35), channel_id=1, source_target_pairs={{0,6},{1,7},{2,4},{3,5},{4,2},{5,3},{6,0},{7,1},{8,14},{9,15},{10,... | collective-permute-start | bytes 159752 | tf_op jit(solution)/shard_map/ppermute | solution.py:374
  15.1 4.7 %copy-start.3 = (f32[1,1024]{1,0:T(1,128)S(1)}, f32[1,1024]{1,0:T(1,128)}, u32[]{:S(2)}) copy-start(f32[1,1024]{1,0:T(1,128)} %decay_ref.3) | copy-start | bytes 12292
  19.7 1.5 %collective-permute-start.6 = (f32[4,104,128]{2,1,0:T(8,128)S(1)}, f32[4,104,128]{2,1,0:T(8,128)S(1)}, u32[]{:S(2)}, u32[]{:S(2)}) collective-permute-start(f32[4,104,128]{2,1,0:T(8,128)S(1)} %pad_maximum_fusion.here_ref), channel_id=1, source_target_pairs={{0,1},{1,0},{2,3},{3,2},{4,5},{5,4},{6,7},{7,6},{8,9},{9,8},{10,11... | collective-permute-start | bytes 638984 | tf_op jit(solution)/shard_map/ppermute | solution.py:374
